TPU v7x, 128 devices: a whole 4x4x4 slice. The times are simulated.
128 devices in a mesh: slab: 32 (over z_hi, x, y), chan: 4 (over z_lo, core).
Axes of the slice: x: 4, y: 4, z: 4 (z_hi: 2, z_lo: 2; z = z_hi * 2 + z_lo), core: 2. Of those that a mesh axis runs over, the one named last changes fastest.
Arguments:
- tokens: bfloat16 [256, 32, 32, 1024], P('slab', None, None, 'chan'), may hold values from -6 to 6
- refine_feat: bfloat16 [1024, 128, 1024], P('slab', None, 'chan'), may hold values from -6 to 6
- refine_dest: int32 [1024, 1], P('slab'), may hold values from 0 to 31; in each aligned block of 32 rows (0 to 31, 32 to 63, ...) at most 2 rows name the same one
- refine_rows: int32 [1024, 128], P('slab'), may hold values from 0 to 8191
- conv_w: float32 [27, 1024], P(None, 'chan'), may hold values from -0.9 to 0.9
- norm_gain: float32 [1024], replicated, may hold values from 0.5 to 1.5
- w_val: bfloat16 [1024, 1024], P(None, 'chan'), may hold values from -0.1875 to 0.1875
- w_gate: bfloat16 [1024, 1024], P(None, 'chan'), may hold values from -0.1875 to 0.1875
- latent_keys: bfloat16 [128, 1024], replicated, may hold values from -70 to 70
- latents: float32 [128, 1024], P(None, 'chan'), may hold values from -6 to 6
Outputs:
- block_out: bfloat16 [256, 32, 32, 1024], P('slab', None, None, 'chan')
- latent_new: float32 [128, 1024], P(None, 'chan')
Inputs may be any that keep to these rules, and one draw needn't show every extreme that they name: `refine_dest`: in the 32 blocks of one slab, no slab is named by more than 2 blocks. `refine_rows`: an index among the destination slab's tokens.
All inputs are finite; a program needn't handle non-finite values.
Results may differ from a plain program's by a relative error of at most 0.0035.
The roundings to bfloat16 on the way count: a program that leaves them out, or rounds other values in their place, can miss the bound.
Values may be sent and summed in bfloat16 or wider, within the bound.
A program may use at most 128 MiB of HBM per device.

v0:
```python
import math

import jax
import jax.numpy as jnp
from jax import lax
from jax.sharding import PartitionSpec as P


def with_halo(value, sides, width):
    for axis, dim in sides:
        size, length = (lax.axis_size(axis), value.shape[dim])
        up = [(i, (i + 1) % size) for i in range(size - 1)]
        down = [(j, i) for i, j in up]
        last = lax.slice_in_dim(value, length - width, length, axis=dim)
        initial = lax.slice_in_dim(value, 0, width, axis=dim)
        before = lax.ppermute(last, axis, up)
        after = lax.ppermute(initial, axis, down)
        value = jnp.concatenate([before, value, after], axis=dim)
    return value


def normalize(values, norm_gain):
    widened = values.astype(jnp.float32)
    meansq = jnp.mean(widened * widened, axis=-1, keepdims=True)
    return (widened * lax.rsqrt(meansq + 1e-06) * norm_gain).astype(jnp.bfloat16)


def project(normed, w_val, w_gate, latent_keys):
    values = jnp.dot(normed, w_val, preferred_element_type=jnp.float32)
    gates = jnp.dot(normed, w_gate, preferred_element_type=jnp.float32)
    gated = (values * jax.nn.sigmoid(gates)).astype(jnp.bfloat16)
    scores = lax.dot_general(
        normed, latent_keys, (((1,), (1,)), ((), ())), preferred_element_type=jnp.float32
    )
    scores = scores * normed.shape[1] ** (-0.5)
    assign = jax.nn.softmax(scores, axis=-1).astype(jnp.bfloat16)
    pooled = lax.dot_general(
        assign, gated, (((0,), (0,)), ((), ())), preferred_element_type=jnp.float32
    )
    weight_total = jnp.sum(assign.astype(jnp.float32), axis=0)
    return (assign, pooled, weight_total)


def project_blocks(normed, w_val, w_gate, latent_keys):
    row_total = normed.shape[0]
    step_rows = math.gcd(row_total, 2048)
    pieces = normed.reshape(row_total // step_rows, step_rows, normed.shape[1])

    def one_block(piece):
        return project(piece, w_val, w_gate, latent_keys)

    assign, pooled, weight_total = lax.map(one_block, pieces)
    return (
        assign.reshape(row_total, assign.shape[-1]),
        jnp.sum(pooled, axis=0),
        jnp.sum(weight_total, axis=0),
    )


def per_device(
    tokens,
    refine_feat,
    refine_dest,
    refine_rows,
    conv_w,
    norm_gain,
    w_val,
    w_gate,
    latent_keys,
    latents,
):
    depth_cells, side_y, side_x, chan_width = tokens.shape
    row_count = depth_cells * side_y * side_x
    slab_count = lax.axis_size("slab")
    block_total, block_rows = refine_rows.shape
    capacity = max(2, (2 * block_total + slab_count - 1) // slab_count)
    targets = refine_dest[:, 0]
    onehot = (targets[:, None] == jnp.arange(slab_count, dtype=jnp.int32)[None, :]).astype(
        jnp.int32
    )
    position = jnp.sum((jnp.cumsum(onehot, axis=0) - 1) * onehot, axis=1)
    slot_index = targets * capacity + position
    send_feat = (
        jnp.zeros((slab_count * capacity, block_rows, chan_width), jnp.bfloat16)
        .at[slot_index]
        .set(refine_feat)
    )
    send_rows = (
        jnp.full((slab_count * capacity, block_rows), row_count, jnp.int32)
        .at[slot_index]
        .set(refine_rows)
    )
    recv_feat, recv_rows = (
        lax.all_to_all(
            send_feat.reshape(slab_count, capacity, block_rows, chan_width),
            "slab",
            split_axis=0,
            concat_axis=0,
            tiled=True,
        ),
        lax.all_to_all(
            send_rows.reshape(slab_count, capacity, block_rows),
            "slab",
            split_axis=0,
            concat_axis=0,
            tiled=True,
        ),
    )
    injected = (
        jnp.zeros((row_count, chan_width), jnp.float32)
        .at[recv_rows.reshape(-1)]
        .add(recv_feat.reshape(-1, chan_width).astype(jnp.float32), mode="drop")
    )
    extended = with_halo(tokens, (("slab", 0),), 1)
    framed = jnp.pad(extended, ((0, 0), (1, 1), (1, 1), (0, 0)))
    mixing = tokens.astype(jnp.float32) + injected.reshape(depth_cells, side_y, side_x, chan_width)
    for depth in range(3):
        for across in range(3):
            for along in range(3):
                mixing = (
                    mixing
                    + framed[
                        depth : depth + depth_cells,
                        across : across + side_y,
                        along : along + side_x,
                    ].astype(jnp.float32)
                    * conv_w[depth * 9 + across * 3 + along]
                )
    mixed = mixing.astype(jnp.bfloat16).reshape(row_count, chan_width)
    whole = lax.all_gather(mixed, "chan", axis=1, tiled=True)
    normed = normalize(whole, norm_gain)
    assign_all, pooled, weight_total = project_blocks(normed, w_val, w_gate, latent_keys)
    pooled, weight_total = (
        lax.psum(pooled.astype(jnp.bfloat16), "slab").astype(jnp.float32),
        lax.psum(weight_total.astype(jnp.bfloat16), "slab").astype(jnp.float32),
    )
    latent_new = latents + pooled / (weight_total[:, None] + 1.0)
    latent_state = latent_new.astype(jnp.bfloat16)
    readback = jnp.dot(assign_all, latent_state, preferred_element_type=jnp.float32)
    block_out = (mixed.astype(jnp.float32) + readback).astype(jnp.bfloat16)
    return (block_out.reshape(depth_cells, side_y, side_x, chan_width), latent_new)


def solution(mesh):
    return jax.shard_map(
        per_device,
        mesh=mesh,
        in_specs=(
            P("slab", None, None, "chan"),
            P("slab", None, "chan"),
            P("slab", None),
            P("slab", None),
            P(None, "chan"),
            P(),
            P(None, "chan"),
            P(None, "chan"),
            P(),
            P(None, "chan"),
        ),
        out_specs=(P("slab", None, None, "chan"), P(None, "chan")),
        check_vma=False,
    )
```

profile of v0, /device:TPU:0, one launch (start us, length us, event | category | flops | bytes accessed | tf_op | source)
XLA Modules:
  0.0 754.3 jit_solution(17535928109217821288)
XLA Ops:
  10.9 10.7 %all-to-all-start = ((s32[32,2,128]{2,1,0:T(2,128)}), s32[32,2,128]{2,1,0:T(2,128)S(1)}, u32[]{:S(2)}, u32[]{:S(2)}) async-start(s32[32,2,128]{2,1,0:T(2,128)} %bitcast.7), calls=%async_computation | async-start | bytes 65536 | tf_op jit(solution)/shard_map/all_to_all | solution.py:101
  32.4 6.2 scatter_fusion
  38.6 11.6 %all-to-all-start.1 = ((bf16[32,2,128,256]{3,2,1,0:T(8,128)(2,1)}), bf16[32,2,128,256]{3,2,1,0:T(8,128)(2,1)}, u32[]{:S(2)}, u32[]{:S(2)}) async-start(bf16[32,2,128,256]{3,2,1,0:T(8,128)(2,1)} %bitcast.105), calls=%async_computation.1 | async-start | bytes 8388608 | tf_op jit(solution)/shard_map/all_to_all | solution.py:94
  50.4 8.6 %select_maximum_fusion = bf16[10,34,34,256]{3,2,1,0:T(8,128)(2,1)} fusion(bf16[1,32,32,256]{3,2,1,0:T(8,128)(2,1)S(1)} %collective-permute-done.1, bf16[8,32,32,256]{3,2,1,0:T(8,128)(2,1)} %param.12, bf16[1,32,32,256]{3,2,1,0:T(8,128)(2,1)S(1)} %collective-permute-done), kind=kLoop, calls=%fused_computation.73 | loop fusion | flops 56227840 | bytes 11161600 | tf_op jit(solution)/shard_map/concatenate | solution.py:18
  59.0 43.0 %all-to-all-done.1 = bf16[32,2,128,256]{3,2,1,0:T(8,128)(2,1)} async-done(((bf16[32,2,128,256]{3,2,1,0:T(8,128)(2,1)}), bf16[32,2,128,256]{3,2,1,0:T(8,128)(2,1)}, u32[]{:S(2)}, u32[]{:S(2)}) %all-to-all-start.1) | async-done | bytes 4194336 | tf_op jit(solution)/shard_map/all_to_all | solution.py:94
  102.0 44.5 %scatter_custom_fusion.2 = f32[8192,256]{1,0:T(8,128)} fusion(s32[8192]{0:T(1024)S(1)} %bitcast.111, bf16[8192,256]{1,0:T(8,128)(2,1)} %bitcast.44, f32[]{:T(128)} %constant.24.clone.1), kind=kCustom, calls=%fused_computation.70 | custom fusion | flops 4194304 | bytes 12582916 | tf_op jit(solution)/shard_map/scatter-add | solution.py:112
  146.4 48.3 %add_convert_fusion = bf16[8,32,32,256]{3,2,1,0:T(8,128)(2,1)} fusion(f32[8,32,32,256]{3,2,1,0:T(8,128)} %bitcast.104, bf16[8,32,32,256]{3,2,1,0:T(8,128)(2,1)} %param.12, bf16[10,34,34,256]{3,2,1,0:T(8,128)(2,1)} %select_maximum_fusion, bf16[1,32,32,256]{3,2,1,0:T(8,128)(2,1)S(1)} %collective-permute-done.1, ...), kind=kLoop, calls=%fused_computation.72 | loop fusion | flops 178257920 | bytes 118516736 | tf_op jit(solution)/shard_map/convert_element_type | solution.py:129
  195.1 150.6 %all-gather.2.cloned.1.call-done = bf16[8192,1024]{1,0:T(8,128)(2,1)} async-done(((bf16[8192,256]{1,0:T(8,128)(2,1)}), bf16[8192,1024]{1,0:T(8,128)(2,1)}) %all-gather.2.cloned.1.call-update) | async-done | bytes 16777232 | tf_op jit(solution)/shard_map/all_gather | solution.py:130
  345.6 7.5 fusion.38
  356.3 8.2 %fusion.40 = bf16[8192,1024]{1,0:T(8,128)(2,1)} fusion(bf16[8192,1024]{1,0:T(8,128)(2,1)S(1)} %copy-done, f32[1024]{0:T(1024)S(1)} %copy-done.3, f32[8192]{0:T(1024)S(1)} %add_rsqrt_fusion), kind=kLoop, calls=%fused_computation.33 | loop fusion | flops 33554432 | bytes 33591296 | tf_op jit(solution)/shard_map/convert_element_type | solution.py:25
  364.5 58.5 %while.14 = (s32[]{:T(128)}, bf16[4,2048,128]{2,1,0:T(8,128)(2,1)S(1)}, f32[4,128,256]{2,1,0:T(8,128)}, f32[4,128]{1,0:T(4,128)S(1)}, bf16[4,2048,1024]{2,1,0:T(...) while((s32[]{:T(128)}, ...), condition=%wide.region_10.11_spmd, body=%wide.region_6.10_spmd.sunk | while | flops 2823548928 | bytes 28749476 | solution.py:52
  364.5 3.8 fusion.106
  368.8 4.9 fusion.108
  373.6 5.1 fusion.109
  383.4 4.9 fusion.108
  388.2 5.1 fusion.109
  393.7 3.8 fusion.106
  398.0 4.9 fusion.108
  402.9 5.1 fusion.109
  412.6 4.9 fusion.108
  417.5 5.1 fusion.109
  424.7 96.6 %psum.15 = bf16[128]{0:T(256)(128)(2,1)S(1)} all-reduce(bf16[128]{0:T(256)(128)(2,1)S(1)} %reduce_sum.60), channel_id=1, replica_groups=mesh['slab'=32,'chan'=4] {'slab'}, use_global_device_ids=true, to_apply=%region_14.15 | all-reduce | flops 128 | bytes 512 | tf_op jit(solution)/shard_map/psum | solution.py:135
  521.3 219.7 %all-reduce.3.cloned.1.call-done = bf16[128,256]{1,0:T(8,128)(2,1)} async-done(((bf16[128,256]{1,0:T(8,128)(2,1)}), bf16[128,256]{1,0:T(8,128)(2,1)}) %all-reduce.3.cloned.1.call-update) | async-done | bytes 65552 | tf_op jit(solution)/shard_map/psum | solution.py:134
  742.0 5.5 fusion.44
  (75 shorter events, 31.5 us)
Async XLA Ops:
  10.9 27.7 %all-to-all-start = ((s32[32,2,128]{2,1,0:T(2,128)}), s32[32,2,128]{2,1,0:T(2,128)S(1)}, u32[]{:S(2)}, u32[]{:S(2)}) async-start(s32[32,2,128]{2,1,0:T(2,128)} %bitcast.7), calls=%async_computation | async-start | bytes 65536 | tf_op jit(solution)/shard_map/all_to_all | solution.py:101
  22.9 27.5 %collective-permute-start = (bf16[1,32,32,256]{3,2,1,0:T(8,128)(2,1)S(1)}, bf16[1,32,32,256]{3,2,1,0:T(8,128)(2,1)S(1)}, u32[]{:S(2)}, u32[]{:S(2)}) collective-permute-start(bf16[1,32,32,256]{3,2,1,0:T(8,128)(2,1)S(1)} %get-tuple-element.69), channel_id=1, source_target_pairs={{0,4},{4,8},{8,12},{12,16},{16,20},{20,24},{24,28},{28,32},{32,36}... | collective-permute-start | bytes 1572872 | tf_op jit(solution)/shard_map/ppermute | solution.py:16
  26.6 23.7 %collective-permute-start.1 = (bf16[1,32,32,256]{3,2,1,0:T(8,128)(2,1)S(1)}, bf16[1,32,32,256]{3,2,1,0:T(8,128)(2,1)S(1)}, u32[]{:S(2)}, u32[]{:S(2)}) collective-permute-start(bf16[1,32,32,256]{3,2,1,0:T(8,128)(2,1)S(1)} %get-tuple-element.70), channel_id=1, source_target_pairs={{4,0},{8,4},{12,8},{16,12},{20,16},{24,20},{28,24},{32,28},{36,32}... | collective-permute-start | bytes 1572872 | tf_op jit(solution)/shard_map/ppermute | solution.py:17
  38.6 63.4 %all-to-all-start.1 = ((bf16[32,2,128,256]{3,2,1,0:T(8,128)(2,1)}), bf16[32,2,128,256]{3,2,1,0:T(8,128)(2,1)}, u32[]{:S(2)}, u32[]{:S(2)}) async-start(bf16[32,2,128,256]{3,2,1,0:T(8,128)(2,1)} %bitcast.105), calls=%async_computation.1 | async-start | bytes 8388608 | tf_op jit(solution)/shard_map/all_to_all | solution.py:94
  50.3 295.4 %all-gather.2.cloned.1.call-start = ((), (), s32[]{:S(2)}) async-start(), calls=%async_computation.2 | async-start | bytes 20971520 | tf_op jit(solution)/shard_map/all_gather | solution.py:130
  194.8 546.2 %all-reduce.3.cloned.1.call-start = ((), (), s32[]{:S(2)}) async-start(), calls=%async_computation.3 | async-start | bytes 131072 | tf_op jit(solution)/shard_map/psum | solution.py:134
  195.1 158.1 %copy-start.3 = (f32[1024]{0:T(1024)S(1)}, f32[1024]{0:T(1024)}, u32[]{:S(2)}) copy-start(f32[1024]{0:T(1024)} %param.17) | copy-start | bytes 12292
  345.6 10.7 %copy-start = (bf16[8192,1024]{1,0:T(8,128)(2,1)S(1)}, bf16[8192,1024]{1,0:T(8,128)(2,1)}, u32[]{:S(2)}) copy-start(bf16[8192,1024]{1,0:T(8,128)(2,1)} %all-gather.2.cloned.1.call-done) | copy-start | bytes 50331652
  356.3 8.2 %copy-start.6 = (bf16[128,1024]{1,0:T(8,128)(2,1)S(1)}, bf16[128,1024]{1,0:T(8,128)(2,1)}, u32[]{:S(2)}) copy-start(bf16[128,1024]{1,0:T(8,128)(2,1)} %param.20) | copy-start | bytes 786436
  364.5 376.5 %copy-start.2 = (f32[128,256]{1,0:T(8,128)S(1)}, f32[128,256]{1,0:T(8,128)}, u32[]{:S(2)}) copy-start(f32[128,256]{1,0:T(8,128)} %param.21) | copy-start | bytes 393220
  364.5 4.2 copy-start.5
  368.7 4.9 copy-start.4
  379.1 4.2 copy-start.5
  383.4 4.9 copy-start.4
  393.7 4.2 copy-start.5
  398.0 4.9 copy-start.4
  408.4 4.2 copy-start.5
  412.6 4.9 copy-start.4
  742.0 5.5 copy-start.1
Sparse Core Ops, SparseCore 0:
  194.9 150.6 all-gather.1
  424.8 316.1 all-reduce.2
where the time goes:
time: 755 us; the launch traced here: 754 us
  waiting for transfers between devices  413 us (55%)
  other arithmetic  124 us (16%)
  blocking collectives  96.6 us (13%)
  matrix products  60.4 us (8%)
  starting transfers between devices  27.7 us (4%)
  local copies, waits for them, and re-layouts  18.1 us (2%)
  between operations  14.2 us (2%)
    psum x1, waiting for transfers between devices, per_device(): lax.psum(pooled.astype(jnp.bfloat16), 'slab').astype(jnp.float32)  220 us
    all_gather x1, waiting for transfers between devices, per_device(): whole = lax.all_gather(mixed, 'chan', axis=1, tiled=True)  151 us
    psum x1, blocking collectives, per_device(): lax.psum(weight_total.astype(jnp.bfloat16), 'slab').astype(jnp.float32)  96.6 us
    convert_element_type x1, other arithmetic, per_device(): mixed = mixing.astype(jnp.bfloat16).reshape(row_count, chan_width)  48.3 us
    scatter-add x1, other arithmetic, per_device(): injected = jnp.zeros((row_count, chan_width), jnp.float32).at[recv_rows.r...  44.5 us
    all_to_all x1, waiting for transfers between devices, per_device(): lax.all_to_all(send_feat.reshape(slab_count, capacity, block_rows, chan_w...  43 us
    dot_general x4, matrix products, project(): lax.dot_general(assign, gated, (((0,), (0,)), ((), ())), preferred_elemen...  20.3 us
    dot_general x4, matrix products, project(): gates = jnp.dot(normed, w_gate, preferred_element_type=jnp.float32)  19.5 us
  transfers between devices with their start and end apart: 6, of which 3 were waited for; matrix products, arithmetic and copies ran while one was open for 3% of the time, Pallas kernels for 0%

commit v1 on v0

v1 whole, which is shorter than its diff:
```python
import functools

import jax
import jax.numpy as jnp
from jax import lax
from jax.experimental import pallas as pl
from jax.experimental.pallas import tpu as pltpu
from jax.sharding import PartitionSpec as P

MESH = pl.DeviceIdType.MESH
BF16 = jnp.bfloat16
F32 = jnp.float32
EXTRA = 8


def whole():
    return pl.BlockSpec(memory_space=pltpu.VMEM)


def pack_kernel(src_ref, feat_ref, code_ref, out_ref):
    slots, rows = out_ref.shape[0], feat_ref.shape[1]

    def one(j, carry):
        out_ref[j, pl.ds(0, rows), :] = feat_ref[src_ref[j]]
        out_ref[j, pl.ds(rows, EXTRA), :] = code_ref[j]
        return carry

    lax.fori_loop(0, slots, one, 0)


def pack(source, feat, code):
    slots = source.shape[0]
    _, rows, width = feat.shape
    return pl.pallas_call(
        pack_kernel,
        out_shape=jax.ShapeDtypeStruct((slots, rows + EXTRA, width), BF16),
        in_specs=[pl.BlockSpec(memory_space=pltpu.SMEM), whole(), whole()],
        out_specs=whole(),
        cost_estimate=pl.CostEstimate(flops=0, bytes_accessed=6 << 20, transcendentals=0),
        name="pack",
    )(source, feat, code)


def conv_kernel(tokens_ref, before_ref, after_ref, w_ref, out_ref, plane):
    z = pl.program_id(0)
    last = pl.num_programs(0) - 1
    depth, side_y, side_x, width = tokens_ref.shape

    def widen(slot, value):
        plane[slot, pl.ds(1, side_y)] = value.astype(F32)

    @pl.when(z == 0)
    def _():
        zero = jnp.zeros((side_x, width), F32)
        for slot in range(3):
            plane[slot, 0] = zero
            plane[slot, side_y + 1] = zero
        widen(2, before_ref[0])
        widen(0, tokens_ref[0])

    ahead = lax.rem(z + 1, 3)

    @pl.when(z < last)
    def _():
        widen(ahead, tokens_ref[z + 1])

    @pl.when(z == last)
    def _():
        widen(ahead, after_ref[0])

    slots = (lax.rem(z + 2, 3), lax.rem(z, 3), ahead)
    column = lax.broadcasted_iota(jnp.int32, (side_x, 128), 0)
    for half in range(width // 128):
        lanes = pl.ds(128 * half, 128)

        def one(y, carry):
            sums = [None, None, None]
            for dz in range(3):
                for dy in range(3):
                    row = plane[slots[dz], y + dy, :, lanes]
                    for dx in range(3):
                        k = 9 * dz + 3 * dy + dx
                        term = row * w_ref[pl.ds(k, 1), lanes]
                        sums[dx] = term if sums[dx] is None else sums[dx] + term
            centre = plane[slots[1], y + 1, :, lanes] + sums[1]
            left = jnp.where(column == 0, 0.0, pltpu.roll(sums[0], 1, 0))
            right = jnp.where(column == side_x - 1, 0.0, pltpu.roll(sums[2], side_x - 1, 0))
            out_ref[pl.ds(pl.multiple_of(y * side_x, side_x), side_x), lanes] = centre + left + right
            return carry

        lax.fori_loop(0, side_y, one, 0)


def conv(tokens, before, after, w):
    depth, side_y, side_x, width = tokens.shape
    rows = side_y * side_x
    fixed = lambda shape: pl.BlockSpec(shape, lambda z: (0,) * len(shape))
    return pl.pallas_call(
        conv_kernel,
        grid=(depth,),
        out_shape=jax.ShapeDtypeStruct((depth * rows, width), F32),
        in_specs=[fixed(tokens.shape), fixed(before.shape), fixed(after.shape), fixed(w.shape)],
        out_specs=pl.BlockSpec((rows, width), lambda z: (z, 0)),
        scratch_shapes=[pltpu.VMEM((3, side_y + 2, side_x, width), F32)],
        cost_estimate=pl.CostEstimate(
            flops=54 * depth * rows * width, bytes_accessed=30 << 20, transcendentals=0
        ),
        name="conv",
    )(tokens, before, after, w)


GROUP = 16


def scatter_kernel(rows_ref, clash_ref, base_ref, recv_ref, out_ref, acc, wide, feat, sems, base_sem):
    slots, block_rows = rows_ref.shape
    total, width = acc.shape
    step = 1024

    base_copy = pltpu.make_async_copy(base_ref, acc, base_sem)
    base_copy.start()

    def fetch(j):
        return pltpu.make_async_copy(
            recv_ref.at[j, pl.ds(0, block_rows)], feat.at[lax.rem(j, 4)], sems.at[lax.rem(j, 4)]
        )

    for j in range(3):
        fetch(j).start()
    base_copy.wait()

    def one(j, carry):
        fetch(j).wait()

        @pl.when(j + 3 < slots)
        def _():
            fetch(j + 3).start()

        @pl.when(rows_ref[j, 0] < total)
        def _():
            wide[...] = feat[lax.rem(j, 4)].astype(F32)

            def group(g, inner):
                first = g * GROUP
                where = [rows_ref[j, first + k] for k in range(GROUP)]
                base = pl.multiple_of(first, GROUP)

                @pl.when(clash_ref[j, g] == 0)
                def _():
                    olds = [acc[pl.ds(r, 1), :] for r in where]
                    news = [
                        old + wide[pl.ds(base + k, 1), :] for k, old in enumerate(olds)
                    ]
                    for r, new in zip(where, news):
                        acc[pl.ds(r, 1), :] = new

                @pl.when(clash_ref[j, g] != 0)
                def _():
                    for k, r in enumerate(where):
                        acc[pl.ds(r, 1), :] = acc[pl.ds(r, 1), :] + wide[pl.ds(base + k, 1), :]

                return inner

            lax.fori_loop(0, block_rows // GROUP, group, 0)

        return carry

    lax.fori_loop(0, slots, one, 0)

    def finish(i, carry):
        part = pl.ds(pl.multiple_of(i * step, step), step)
        out_ref[part, :] = acc[part, :].astype(BF16)
        return carry

    lax.fori_loop(0, total // step, finish, 0)


def scatter(rows, clash, base, recv):
    total, width = base.shape
    block_rows = rows.shape[1]
    return pl.pallas_call(
        scatter_kernel,
        out_shape=jax.ShapeDtypeStruct((total, width), BF16),
        in_specs=[
            pl.BlockSpec(memory_space=pltpu.SMEM),
            pl.BlockSpec(memory_space=pltpu.SMEM),
            pl.BlockSpec(memory_space=pl.ANY),
            pl.BlockSpec(memory_space=pl.ANY),
        ],
        out_specs=whole(),
        scratch_shapes=[
            pltpu.VMEM((total, width), F32),
            pltpu.VMEM((block_rows, width), F32),
            pltpu.VMEM((4, block_rows, width), BF16),
            pltpu.SemaphoreType.DMA((4,)),
            pltpu.SemaphoreType.DMA,
        ],
        cost_estimate=pl.CostEstimate(flops=2 << 20, bytes_accessed=16 << 20, transcendentals=0),
        name="scatter",
    )(rows, clash, base, recv)


CHUNKS = 8


def mix_kernel(
    mixed_ref,
    w_ref,
    keys_ref,
    gain_ref,
    latents_ref,
    assign_ref,
    latent_ref,
    xbuf,
    nbuf,
    wbuf,
    own,
    pooled,
    totals,
    part_out,
    part_in,
    tile_out,
    tile_in,
    new_out,
    new_in,
    local_sem,
    x_send,
    x_recv,
    w_send,
    w_recv,
    a_send,
    a_recv,
    p_send,
    p_recv,
    t_send,
    t_recv,
    n_send,
    n_recv,
):
    slab = lax.axis_index("slab")
    chan = lax.axis_index("chan")
    slabs = lax.axis_size("slab")
    z_lo, core = chan // 2, chan % 2
    peers = (
        chan,
        z_lo * 2 + (1 - core),
        (1 - z_lo) * 2 + core,
        (1 - z_lo) * 2 + (1 - core),
    )
    far_slab = (slab + slabs // 2) % slabs
    quarter = xbuf.shape[1]
    size = quarter // CHUNKS
    width = xbuf.shape[2]
    count = slabs - 1

    def local_copies():
        yield pltpu.make_async_copy(
            mixed_ref.at[pl.ds(chan * quarter, quarter)], xbuf.at[chan], local_sem.at[0]
        )
        yield pltpu.make_async_copy(w_ref, wbuf.at[chan], local_sem.at[1])

    for copy in local_copies():
        copy.start()

    barrier = pltpu.get_barrier_semaphore()
    for d in (1, 2, 3):
        pl.semaphore_signal(barrier, inc=1, device_id=(slab, peers[d]), device_id_type=MESH)
    pl.semaphore_signal(barrier, inc=1, device_id=(far_slab, peers[2]), device_id_type=MESH)

    def greet(k, carry):
        pl.semaphore_signal(
            barrier, inc=1, device_id=((slab + k) % slabs, chan), device_id_type=MESH
        )
        return carry

    lax.fori_loop(1, slabs, greet, 0)
    pl.semaphore_wait(barrier, 4 + count)

    def x_copy(d, i):
        rows = pl.ds(i * size, size)
        return pltpu.make_async_remote_copy(
            src_ref=mixed_ref.at[pl.ds(peers[d] * quarter + i * size, size)],
            dst_ref=xbuf.at[chan, rows],
            send_sem=x_send.at[d - 1, i],
            recv_sem=x_recv.at[d - 1, i],
            device_id=(slab, peers[d]),
            device_id_type=MESH,
        )

    def w_copy(which):
        source, device = (
            (w_ref, (slab, peers[1])),
            (w_ref, (far_slab, peers[2])),
            (wbuf.at[peers[2]], (slab, peers[1])),
        )[which]
        return pltpu.make_async_remote_copy(
            src_ref=source,
            dst_ref=wbuf.at[peers[2] if which == 2 else chan],
            send_sem=w_send.at[which],
            recv_sem=w_recv.at[which],
            device_id=device,
            device_id_type=MESH,
        )

    def a_copy(d, i):
        rows = pl.ds(chan * quarter + i * size, size)
        return pltpu.make_async_remote_copy(
            src_ref=own.at[pl.ds(i * size, size)],
            dst_ref=assign_ref.at[rows],
            send_sem=a_send.at[d - 1, i],
            recv_sem=a_recv.at[d - 1, i],
            device_id=(slab, peers[d]),
            device_id_type=MESH,
        )

    def start_x(i, carry):
        for d in (1, 2, 3):
            x_copy(d, i).start()
        return carry

    w_copy(1).start()
    lax.fori_loop(0, CHUNKS, start_x, 0)
    w_copy(0).start()
    pooled[...] = jnp.zeros_like(pooled)
    totals[...] = jnp.zeros_like(totals)
    for copy in local_copies():
        copy.wait()

    def assign_chunk(i):
        for d in (1, 2, 3):
            x_copy(d, i).wait_recv()
        rows = pl.ds(pl.multiple_of(i * size, size), size)
        wide = [xbuf[p, rows, :].astype(F32) for p in range(4)]
        square = sum(jnp.sum(v * v, axis=1, keepdims=True) for v in wide)
        scale = lax.rsqrt(square * (1.0 / (4 * width)) + 1e-06)
        for p in range(4):
            lanes = pl.ds(p * width, width)
            nbuf[rows, lanes] = (wide[p] * scale * gain_ref[:, lanes]).astype(BF16)
        scores = lax.dot_general(
            nbuf[rows, :], keys_ref[...], (((1,), (1,)), ((), ())), preferred_element_type=F32
        )
        scores = scores * (4 * width) ** (-0.5)
        top = jnp.max(scores, axis=1, keepdims=True)
        power = jnp.exp(scores - top)
        own[rows, :] = (power / jnp.sum(power, axis=1, keepdims=True)).astype(BF16)
        for d in (1, 2):
            a_copy(d, i).start()

    def pool_chunk(i):
        rows = pl.ds(pl.multiple_of(i * size, size), size)
        assign = own[rows, :]
        ones = jnp.ones((size, 128), BF16)
        over_rows = (((0,), (0,)), ((), ()))
        totals[...] += lax.dot_general(assign, ones, over_rows, preferred_element_type=F32)
        for p in range(4):
            both = jnp.dot(nbuf[rows, :], wbuf[p], preferred_element_type=F32)
            gated = (both[:, :width] * jax.nn.sigmoid(both[:, width:])).astype(BF16)
            pooled[p] += lax.dot_general(assign, gated, over_rows, preferred_element_type=F32)

    def early(i, carry):
        assign_chunk(i)
        return carry

    lax.fori_loop(0, CHUNKS // 2, early, 0)
    w_copy(1).wait_recv()
    w_copy(2).start()
    w_copy(0).wait_recv()
    w_copy(2).wait_recv()

    def late(i, carry):
        assign_chunk(i + CHUNKS // 2)
        pool_chunk(2 * i)
        pool_chunk(2 * i + 1)
        return carry

    lax.fori_loop(0, CHUNKS // 2, late, 0)

    keep = pltpu.make_async_copy(own, assign_ref.at[pl.ds(chan * quarter, quarter)], local_sem.at[0])
    keep.start()

    def p_copy(d):
        return pltpu.make_async_remote_copy(
            src_ref=part_out.at[peers[d]],
            dst_ref=part_in.at[d - 1],
            send_sem=p_send.at[d - 1],
            recv_sem=p_recv.at[d - 1],
            device_id=(slab, peers[d]),
            device_id_type=MESH,
        )

    for p in range(4):
        part_out[p, :, pl.ds(0, width)] = pooled[p].astype(BF16)
        part_out[p, :, pl.ds(width, 128)] = totals[...].astype(BF16)
    for d in (2, 3, 1):
        p_copy(d).start()
    for d in (1, 2, 3):
        p_copy(d).wait_recv()
    mine = pooled[chan]
    weight = totals[...]
    for d in range(3):
        mine = mine + part_in[d, :, pl.ds(0, width)].astype(F32)
        weight = weight + part_in[d, :, pl.ds(width, 128)].astype(F32)

    for t in range(slabs):
        tile = (slice(8 * (t // 2), 8 * (t // 2) + 8), slice(128 * (t % 2), 128 * (t % 2) + 128))
        tile_out[t, 0] = mine[tile]
        tile_out[t, 1] = weight[tile[0]]

    def t_copy(k):
        to = (slab + k) % slabs
        return pltpu.make_async_remote_copy(
            src_ref=tile_out.at[to],
            dst_ref=tile_in.at[slab],
            send_sem=t_send.at[k - 1],
            recv_sem=t_recv.at[k - 1],
            device_id=(to, chan),
            device_id_type=MESH,
        )

    def n_copy(k):
        return pltpu.make_async_remote_copy(
            src_ref=new_out,
            dst_ref=new_in.at[slab],
            send_sem=n_send.at[k - 1],
            recv_sem=n_recv.at[k - 1],
            device_id=((slab + k) % slabs, chan),
            device_id_type=MESH,
        )

    def over_peers(action):
        def body(k, carry):
            action(k)
            return carry

        lax.fori_loop(1, slabs, body, 0)

    over_peers(lambda k: t_copy(k).start())
    tile_in[slab] = tile_out[slab]
    over_peers(lambda k: t_copy(k).wait_recv())
    sums = jnp.sum(tile_in[...], axis=0)
    held = latents_ref[
        pl.ds(pl.multiple_of(8 * (slab // 2), 8), 8), pl.ds(pl.multiple_of(128 * (slab % 2), 128), 128)
    ]
    fresh = held + sums[0] / (sums[1] + 1.0)
    new_out[...] = fresh
    over_peers(lambda k: n_copy(k).start())
    new_in[slab] = fresh

    def forward():
        rows = pl.ds(peers[2] * quarter, quarter)
        return pltpu.make_async_remote_copy(
            src_ref=assign_ref.at[rows],
            dst_ref=assign_ref.at[rows],
            send_sem=a_send.at[2, 0],
            recv_sem=a_recv.at[2, 0],
            device_id=(slab, peers[1]),
            device_id_type=MESH,
        )

    def landed(i, carry):
        a_copy(2, i).wait_recv()
        return carry

    lax.fori_loop(0, CHUNKS, landed, 0)
    forward().start()

    over_peers(lambda k: n_copy(k).wait_recv())
    for t in range(slabs):
        latent_ref[8 * (t // 2) : 8 * (t // 2) + 8, 128 * (t % 2) : 128 * (t % 2) + 128] = new_in[t]

    def drained(i, carry):
        a_copy(1, i).wait_recv()
        for d in (1, 2):
            a_copy(d, i).wait_send()
        for d in (1, 2, 3):
            x_copy(d, i).wait_send()
        return carry

    lax.fori_loop(0, CHUNKS, drained, 0)
    for which in range(3):
        w_copy(which).wait_send()
    for d in (1, 2, 3):
        p_copy(d).wait_send()
    over_peers(lambda k: t_copy(k).wait_send())
    over_peers(lambda k: n_copy(k).wait_send())
    forward().wait()
    keep.wait()


def mix(mixed, weights, keys, gain, latents):
    rows, width = mixed.shape
    slabs = lax.axis_size("slab")
    quarter = rows // 4
    held = latents.shape[0]
    dma = pltpu.SemaphoreType.DMA
    return pl.pallas_call(
        mix_kernel,
        out_shape=(
            jax.ShapeDtypeStruct((rows, held), BF16),
            jax.ShapeDtypeStruct((held, width), F32),
        ),
        in_specs=[
            pl.BlockSpec(memory_space=pl.ANY),
            pl.BlockSpec(memory_space=pl.ANY),
            whole(),
            whole(),
            whole(),
        ],
        out_specs=(pl.BlockSpec(memory_space=pl.ANY), whole()),
        scratch_shapes=[
            pltpu.VMEM((4, quarter, width), BF16),
            pltpu.VMEM((quarter, 4 * width), BF16),
            pltpu.VMEM((4,) + weights.shape, BF16),
            pltpu.VMEM((quarter, held), BF16),
            pltpu.VMEM((4, held, width), F32),
            pltpu.VMEM((held, 128), F32),
            pltpu.VMEM((4, held, width + 128), BF16),
            pltpu.VMEM((3, held, width + 128), BF16),
            pltpu.VMEM((slabs, 2, 8, 128), F32),
            pltpu.VMEM((slabs, 2, 8, 128), F32),
            pltpu.VMEM((8, 128), F32),
            pltpu.VMEM((slabs, 8, 128), F32),
            dma((2,)),
            dma((3, CHUNKS)),
            dma((3, CHUNKS)),
            dma((3,)),
            dma((3,)),
            dma((3, CHUNKS)),
            dma((3, CHUNKS)),
            dma((3,)),
            dma((3,)),
            dma((slabs - 1,)),
            dma((slabs - 1,)),
            dma((slabs - 1,)),
            dma((slabs - 1,)),
        ],
        compiler_params=pltpu.CompilerParams(
            collective_id=0, has_side_effects=True, vmem_limit_bytes=48 << 20
        ),
        cost_estimate=pl.CostEstimate(flops=10 << 30, bytes_accessed=16 << 20, transcendentals=0),
        name="mix",
    )(mixed, weights, keys, gain, latents)


def per_device(
    tokens,
    refine_feat,
    refine_dest,
    refine_rows,
    conv_w,
    norm_gain,
    w_val,
    w_gate,
    latent_keys,
    latents,
):
    depth, side_y, side_x, width = tokens.shape
    row_count = depth * side_y * side_x
    slabs = lax.axis_size("slab")
    blocks, block_rows = refine_rows.shape
    capacity = max(2, (2 * blocks + slabs - 1) // slabs)
    slots = slabs * capacity

    targets = refine_dest[:, 0]
    ids = jnp.arange(blocks, dtype=jnp.int32)
    earlier = (targets[None, :] == targets[:, None]) & (ids[None, :] < ids[:, None])
    position = targets * capacity + jnp.sum(earlier.astype(jnp.int32), axis=1)
    chosen = position[None, :] == jnp.arange(slots, dtype=jnp.int32)[:, None]
    source = jnp.sum(jnp.where(chosen, ids[None, :], 0), axis=1)
    filled = jnp.any(chosen, axis=1)
    wanted = jnp.where(filled[:, None], refine_rows[source], row_count)
    code = jnp.concatenate([wanted // 128, wanted % 128], axis=1).astype(BF16)
    code = jnp.broadcast_to(code[:, None, :], (slots, EXTRA, width))

    up = [(i, i + 1) for i in range(slabs - 1)]
    down = [(i + 1, i) for i in range(slabs - 1)]
    before = lax.ppermute(tokens[-1:], "slab", up)
    after = lax.ppermute(tokens[:1], "slab", down)

    sent = pack(source, refine_feat, code)
    sent, before, after = lax.optimization_barrier((sent, before, after))
    received = lax.all_to_all(
        sent.reshape(slabs, capacity * (block_rows + EXTRA), width),
        "slab",
        split_axis=0,
        concat_axis=0,
        tiled=True,
    ).reshape(slots, block_rows + EXTRA, width)

    base = conv(tokens, before, after, conv_w)
    weights = jnp.concatenate([w_val, w_gate], axis=1)

    got = received[:, block_rows, :].astype(jnp.int32)
    rows = got[:, :block_rows] * 128 + got[:, block_rows:]
    grouped = rows.reshape(slots, block_rows // GROUP, GROUP)
    same = grouped[..., :, None] == grouped[..., None, :]
    above = jnp.arange(GROUP)[:, None] < jnp.arange(GROUP)[None, :]
    clash = jnp.any(same & above, axis=(2, 3)).astype(jnp.int32)

    mixed = scatter(rows, clash, base, received)
    assign, latent_new = mix(mixed, weights, latent_keys, norm_gain[None, :], latents)
    readback = jnp.dot(assign, latent_new.astype(BF16), preferred_element_type=F32)
    block_out = (mixed.astype(F32) + readback).astype(BF16)
    return (block_out.reshape(depth, side_y, side_x, width), latent_new)


def solution(mesh):
    return jax.shard_map(
        per_device,
        mesh=mesh,
        in_specs=(
            P("slab", None, None, "chan"),
            P("slab", None, "chan"),
            P("slab", None),
            P("slab", None),
            P(None, "chan"),
            P(),
            P(None, "chan"),
            P(None, "chan"),
            P(),
            P(None, "chan"),
        ),
        out_specs=(P("slab", None, None, "chan"), P(None, "chan")),
        check_vma=False,
    )
```

time: 755 us -> 251 us (0.33)
  waiting for transfers between devices: 413 us -> 34.8 us
  Pallas kernels: 0 us -> 183 us
  other arithmetic: 124 us -> 3.19 us
  blocking collectives: 96.6 us -> 0 us
  matrix products: 60.4 us -> 3.25 us
  between operations: 14.2 us -> 0.85 us
  local copies, waits for them, and re-layouts: 18.1 us -> 4.89 us
  starting transfers between devices: 27.7 us -> 19.5 us
    psum x1 -> x0, waiting for transfers between devices: 220 us -> none  [per_device(): lax.psum(pooled.astype(jnp.bfloat16), 'slab').astype(jnp.float32)]
    pallas_call x0 -> x4, Pallas kernels: none -> 183 us  [the longest x1 82.2 us: mix(): pl.pallas_call(mix_kernel, out_shape=(jax.ShapeDtypeStruct((rows, held),...]
    all_gather x1 -> x0, waiting for transfers between devices: 151 us -> none  [per_device(): whole = lax.all_gather(mixed, 'chan', axis=1, tiled=True)]
    psum x1 -> x0, blocking collectives: 96.6 us -> none  [per_device(): lax.psum(weight_total.astype(jnp.bfloat16), 'slab').astype(jnp.float32)]
    dot_general x13 -> x1, matrix products: 60.4 us -> 3.25 us  [per_device(): jnp.dot(assign, latent_new.astype(BF16), preferred_element_type=F32)]
    convert_element_type x3 -> x2, other arithmetic: 57.2 us -> 1.01 us  [the longest x1 1 us: per_device(): got = received[:, block_rows, :].astype(jnp.int32)]
    scatter-add x1 -> x0, other arithmetic: 44.5 us -> none  [per_device(): injected = jnp.zeros((row_count, chan_width), jnp.float32).at[recv_rows.r...]
    all_to_all x2 -> x1, waiting for transfers between devices: 43 us -> 28.3 us  [per_device(): lax.all_to_all(sent.reshape(slabs, capacity * (block_rows + EXTRA), width...]
  transfers between devices with their start and end apart: 6 -> 3, of which waited for: 3 -> 3; matrix products, arithmetic and copies ran while one was open for 3% -> 1% of each run, Pallas kernels for 0% -> 12%
where the time goes in v1:
time: 251 us; the launch traced here: 250 us
  Pallas kernels  183 us (73%)
  waiting for transfers between devices  34.8 us (14%)
  starting transfers between devices  19.5 us (8%)
  local copies, waits for them, and re-layouts  4.89 us (2%)
  matrix products  3.25 us (1%)
  other arithmetic  3.19 us (1%)
    pallas_call x1, Pallas kernels, mix(): pl.pallas_call(mix_kernel, out_shape=(jax.ShapeDtypeStruct((rows, held),...  82.2 us
    pallas_call x1, Pallas kernels, scatter(): pl.pallas_call(scatter_kernel, out_shape=jax.ShapeDtypeStruct((total, wid...  70.3 us
    all_to_all x1, waiting for transfers between devices, per_device(): lax.all_to_all(sent.reshape(slabs, capacity * (block_rows + EXTRA), width...  28.3 us
    pallas_call x1, Pallas kernels, conv(): pl.pallas_call(conv_kernel, grid=(depth,), out_shape=jax.ShapeDtypeStruct...  26.3 us
    all_to_all x1, starting transfers between devices, per_device(): lax.all_to_all(sent.reshape(slabs, capacity * (block_rows + EXTRA), width...  14.6 us
  transfers between devices with their start and end apart: 3, of which 3 were waited for; matrix products, arithmetic and copies ran while one was open for 1% of the time, Pallas kernels for 12%

profile of v1, /device:TPU:0, one launch (start us, length us, event | category | flops | bytes accessed | tf_op | source)
XLA Modules:
  0.0 249.5 jit_solution(4811953726148402102)
XLA Ops:
  0.6 1.3 fusion.9
  1.9 3.6 %collective-permute-start = (bf16[1,32,32,256]{3,2,1,0:T(8,128)(2,1)S(1)}, bf16[1,32,32,256]{3,2,1,0:T(8,128)(2,1)S(1)}, u32[]{:S(2)}, u32[]{:S(2)}) collective-permute-start(bf16[1,32,32,256]{3,2,1,0:T(8,128)(2,1)S(1)} %get-tuple-element.13), channel_id=1, source_target_pairs={{0,4},{4,8},{8,12},{12,16},{16,20},{20,24},{24,28},{28,32},{32,36}... | collective-permute-start | bytes 1572872 | tf_op jit(solution)/shard_map/ppermute | solution.py:577
  5.6 1.3 collective-permute-start.1
  6.9 0.9 convert_reduce_fusion
  7.8 0.7 multiply_add_fusion
  8.4 0.1 select_reduce_fusion.src_ref
  8.6 0.6 gather_fusion
  9.2 0.1 fusion.6
  9.3 0.1 fusion.2
  9.4 0.7 broadcast_in_dim.47.code_ref
  10.1 4.2 %pack.1 = bf16[64,136,256]{2,1,0:T(8,128)(2,1)} custom-call(s32[64]{0:T(128)} %copy-done.10, bf16[32,128,256]{2,1,0:T(8,128)(2,1)} %feat_ref.1, bf16[64,8,256]{2,1,0:T(8,128)(2,1)} %broadcast_in_dim.47.code_ref), custom_call_target="tpu_custom_call" | custom-call | bytes 6291456 | tf_op jit(solution)/shard_map/pack/pallas_call | solution.py:34
  14.3 2.4 collective-permute-done.before_ref
  16.7 4.1 %collective-permute-done.1.after_ref = bf16[1,32,32,256]{3,2,1,0:T(8,128)(2,1)S(1)} collective-permute-done((bf16[1,32,32,256]{3,2,1,0:T(8,128)(2,1)S(1)}, bf16[1,32,32,256]{3,2,1,0:T(8,128)(2,1)S(1)}, u32[]{:S(2)}, u32[]{:S(2)}) %collective-permute-start.1) | collective-permute-done | bytes 524320 | tf_op jit(solution)/shard_map/ppermute | solution.py:578
  20.8 0.8 copy-done.8
  21.6 14.6 %all-to-all-start = ((bf16[32,272,256]{2,1,0:T(8,128)(2,1)}), bf16[32,272,256]{2,1,0:T(8,128)(2,1)}, u32[]{:S(2)}, u32[]{:S(2)}) async-start(bf16[32,272,256]{2,1,0:T(8,128)(2,1)} %bitcast.16), calls=%async_computation | async-start | bytes 8912896 | tf_op jit(solution)/shard_map/all_to_all | solution.py:582
  36.3 26.3 %conv.1.base_ref = f32[8192,256]{1,0:T(8,128)} custom-call(bf16[8,32,32,256]{3,2,1,0:T(8,128)(2,1)} %tokens_ref.1, bf16[1,32,32,256]{3,2,1,0:T(8,128)(2,1)} %copy-done.7, bf16[1,32,32,256]{3,2,1,0:T(8,128)(2,1)} %copy-done.8, f32[27,256]{1,0:T(8,128)} %w_ref.1), custom_call_target="tpu_custom_call" | custom-call | flops 113246208 | bytes 31457280 | tf_op jit(solution)/shard_map/conv/pallas_call | solution.py:98
  62.7 28.3 %all-to-all-done = bf16[32,272,256]{2,1,0:T(8,128)(2,1)} async-done(((bf16[32,272,256]{2,1,0:T(8,128)(2,1)}), bf16[32,272,256]{2,1,0:T(8,128)(2,1)}, u32[]{:S(2)}, u32[]{:S(2)}) %all-to-all-start) | async-done | bytes 4456480 | tf_op jit(solution)/shard_map/all_to_all | solution.py:582
  90.9 1.0 slice_convert_fusion
  92.1 0.2 and_reduce_fusion
  92.3 0.7 copy.18.clash_ref
  93.0 70.3 %scatter.1.mixed_ref = bf16[8192,256]{1,0:T(8,128)(2,1)} custom-call(s32[64,128]{1,0:T(8,128)} %copy-done.9, s32[64,8]{1,0:T(8,128)} %copy.18.clash_ref, f32[8192,256]{1,0:T(8,128)} %conv.1.base_ref, bf16[64,136,256]{2,1,0:T(8,128)(2,1)} %bitcast.4.recv_ref), custom_call_target="tpu_custom_call" | custom-call | flops 2097152 | bytes 16777216 | tf_op jit(solution)/shard_map/scatter/pallas_call | solution.py:181
  163.4 82.2 %mix.1 = (bf16[8192,128]{1,0:T(8,128)(2,1)S(1)}, f32[128,256]{1,0:T(8,128)S(1)}) custom-call(bf16[8192,256]{1,0:T(8,128)(2,1)} %scatter.1.mixed_ref, bf16[1024,512]{1,0:T(8,128)(2,1)S(1)} %pad_maximum_fusion.w_ref, bf16[128,1024]{1,0:T(8,128)(2,1)S(1)} %copy-done.1, f32[1,1024]{1,0:T(1,128)S(1)} %bitcast.15, f32[128,256]{1,0:T(8,128)S(1)} %copy-done.2), custom_call_target="tpu_custom_call" | custom-call | flops 10737418240 | bytes 16777216 | tf_op jit(solution)/shard_map/mix/pallas_call | solution.py:496
  245.6 3.3 %fusion = bf16[8192,256]{1,0:T(8,128)(2,1)} fusion(bf16[8192,128]{1,0:T(8,128)(2,1)S(1)} %get-tuple-element.10, bf16[8192,256]{1,0:T(8,128)(2,1)S(1)} %copy-done.4, f32[128,256]{1,0:T(8,128)S(1)} %get-tuple-element.19), kind=kOutput, calls=%fused_computation.2 | convolution fusion | flops 543195136 | bytes 10616832 | tf_op jit(solution)/shard_map/dot_general | solution.py:602
  248.8 0.7 copy.23
  (30 shorter events, 0.3 us)
Async XLA Ops:
  0.6 7.9 %copy-start = (s32[32,128]{1,0:T(8,128)S(1)}, s32[32,128]{1,0:T(8,128)}, u32[]{:S(2)}) copy-start(s32[32,128]{1,0:T(8,128)} %param.13) | copy-start | bytes 49156
  1.9 14.8 %collective-permute-start = (bf16[1,32,32,256]{3,2,1,0:T(8,128)(2,1)S(1)}, bf16[1,32,32,256]{3,2,1,0:T(8,128)(2,1)S(1)}, u32[]{:S(2)}, u32[]{:S(2)}) collective-permute-start(bf16[1,32,32,256]{3,2,1,0:T(8,128)(2,1)S(1)} %get-tuple-element.13), channel_id=1, source_target_pairs={{0,4},{4,8},{8,12},{12,16},{16,20},{20,24},{24,28},{28,32},{32,36}... | collective-permute-start | bytes 1572872 | tf_op jit(solution)/shard_map/ppermute | solution.py:577
  5.6 15.3 %collective-permute-start.1 = (bf16[1,32,32,256]{3,2,1,0:T(8,128)(2,1)S(1)}, bf16[1,32,32,256]{3,2,1,0:T(8,128)(2,1)S(1)}, u32[]{:S(2)}, u32[]{:S(2)}) collective-permute-start(bf16[1,32,32,256]{3,2,1,0:T(8,128)(2,1)S(1)} %get-tuple-element.12), channel_id=1, source_target_pairs={{4,0},{8,4},{12,8},{16,12},{20,16},{24,20},{28,24},{32,28},{36,32}... | collective-permute-start | bytes 1572872 | tf_op jit(solution)/shard_map/ppermute | solution.py:578
  8.5 1.6 copy-start.10
  16.7 4.2 %copy-start.7 = (bf16[1,32,32,256]{3,2,1,0:T(8,128)(2,1)}, bf16[1,32,32,256]{3,2,1,0:T(8,128)(2,1)S(1)}, u32[]{:S(2)}) copy-start(bf16[1,32,32,256]{3,2,1,0:T(8,128)(2,1)S(1)} %collective-permute-done.before_ref) | copy-start | bytes 1572868
  20.8 0.8 copy-start.8
  20.8 15.4 %copy-start.5 = (bf16[1024,256]{1,0:T(8,128)(2,1)S(1)}, bf16[1024,256]{1,0:T(8,128)(2,1)}, u32[]{:S(2)}) copy-start(bf16[1024,256]{1,0:T(8,128)(2,1)} %param.17) | copy-start | bytes 1572868
  20.8 15.4 %copy-start.6 = (bf16[1024,256]{1,0:T(8,128)(2,1)S(1)}, bf16[1024,256]{1,0:T(8,128)(2,1)}, u32[]{:S(2)}) copy-start(bf16[1024,256]{1,0:T(8,128)(2,1)} %param.16) | copy-start | bytes 1572868
  21.6 69.3 %all-to-all-start = ((bf16[32,272,256]{2,1,0:T(8,128)(2,1)}), bf16[32,272,256]{2,1,0:T(8,128)(2,1)}, u32[]{:S(2)}, u32[]{:S(2)}) async-start(bf16[32,272,256]{2,1,0:T(8,128)(2,1)} %bitcast.16), calls=%async_computation | async-start | bytes 8912896 | tf_op jit(solution)/shard_map/all_to_all | solution.py:582
  92.0 1.0 copy-start.9
  93.0 70.3 %copy-start.1 = (bf16[128,1024]{1,0:T(8,128)(2,1)S(1)}, bf16[128,1024]{1,0:T(8,128)(2,1)}, u32[]{:S(2)}) copy-start(bf16[128,1024]{1,0:T(8,128)(2,1)} %keys_ref.1) | copy-start | bytes 786436
  93.0 70.3 %copy-start.2 = (f32[128,256]{1,0:T(8,128)S(1)}, f32[128,256]{1,0:T(8,128)}, u32[]{:S(2)}) copy-start(f32[128,256]{1,0:T(8,128)} %latents_ref.1) | copy-start | bytes 393220
  93.0 70.3 %copy-start.3 = (f32[1024]{0:T(1024)S(1)}, f32[1024]{0:T(1024)}, u32[]{:S(2)}) copy-start(f32[1024]{0:T(1024)} %param.15) | copy-start | bytes 12292
  163.4 82.2 %copy-start.4 = (bf16[8192,256]{1,0:T(8,128)(2,1)S(1)}, bf16[8192,256]{1,0:T(8,128)(2,1)}, u32[]{:S(2)}) copy-start(bf16[8192,256]{1,0:T(8,128)(2,1)} %scatter.1.mixed_ref) | copy-start | bytes 12582916

commit v2 on v1

--- a/solution.py
+++ b/solution.py
@@ -17,28 +17,48 @@
     return pl.BlockSpec(memory_space=pltpu.VMEM)
 
 
-def pack_kernel(src_ref, feat_ref, code_ref, out_ref):
-    slots, rows = out_ref.shape[0], feat_ref.shape[1]
-
-    def one(j, carry):
-        out_ref[j, pl.ds(0, rows), :] = feat_ref[src_ref[j]]
-        out_ref[j, pl.ds(rows, EXTRA), :] = code_ref[j]
-        return carry
-
-    lax.fori_loop(0, slots, one, 0)
-
-
-def pack(source, feat, code):
-    slots = source.shape[0]
+def pack_kernel(capacity, empty, dest_ref, feat_ref, rows_ref, out_ref, taken):
+    slots, width = out_ref.shape[0], out_ref.shape[2]
+    blocks, rows, _ = feat_ref.shape
+
+    def coded(number):
+        both = jnp.concatenate([number // 128, number % 128], axis=1)
+        return jnp.broadcast_to(both.astype(F32), (EXTRA, width)).astype(BF16)
+
+    nothing = coded(jnp.full((1, rows), empty, jnp.int32))
+
+    def clear(j, carry):
+        out_ref[j, pl.ds(0, rows), :] = jnp.zeros((rows, width), BF16)
+        out_ref[j, pl.ds(rows, EXTRA), :] = nothing
+        return carry
+
+    lax.fori_loop(0, slots, clear, 0)
+    for t in range(slots // capacity):
+        taken[t] = 0
+
+    def one(b, carry):
+        to = dest_ref[b]
+        slot = to * capacity + taken[to]
+        taken[to] = taken[to] + 1
+        out_ref[slot, pl.ds(0, rows), :] = feat_ref[b]
+        out_ref[slot, pl.ds(rows, EXTRA), :] = coded(rows_ref[pl.ds(b, 1), :])
+        return carry
+
+    lax.fori_loop(0, blocks, one, 0)
+
+
+def pack(dest, feat, row_ids, slabs, capacity, empty):
     _, rows, width = feat.shape
+    slots = slabs * capacity
     return pl.pallas_call(
-        pack_kernel,
+        functools.partial(pack_kernel, capacity, empty),
         out_shape=jax.ShapeDtypeStruct((slots, rows + EXTRA, width), BF16),
         in_specs=[pl.BlockSpec(memory_space=pltpu.SMEM), whole(), whole()],
         out_specs=whole(),
+        scratch_shapes=[pltpu.SMEM((slabs,), jnp.int32)],
         cost_estimate=pl.CostEstimate(flops=0, bytes_accessed=6 << 20, transcendentals=0),
         name="pack",
-    )(source, feat, code)
+    )(dest, feat, row_ids)
 
 
 def conv_kernel(tokens_ref, before_ref, after_ref, w_ref, out_ref, plane):
@@ -85,7 +105,7 @@
             centre = plane[slots[1], y + 1, :, lanes] + sums[1]
             left = jnp.where(column == 0, 0.0, pltpu.roll(sums[0], 1, 0))
             right = jnp.where(column == side_x - 1, 0.0, pltpu.roll(sums[2], side_x - 1, 0))
-            out_ref[pl.ds(pl.multiple_of(y * side_x, side_x), side_x), lanes] = centre + left + right
+            out_ref[half, pl.ds(pl.multiple_of(y * side_x, side_x), side_x), :] = centre + left + right
             return carry
 
         lax.fori_loop(0, side_y, one, 0)
@@ -98,9 +118,9 @@
     return pl.pallas_call(
         conv_kernel,
         grid=(depth,),
-        out_shape=jax.ShapeDtypeStruct((depth * rows, width), F32),
+        out_shape=jax.ShapeDtypeStruct((width // 128, depth * rows, 128), F32),
         in_specs=[fixed(tokens.shape), fixed(before.shape), fixed(after.shape), fixed(w.shape)],
-        out_specs=pl.BlockSpec((rows, width), lambda z: (z, 0)),
+        out_specs=pl.BlockSpec((width // 128, rows, 128), lambda z: (0, z, 0)),
         scratch_shapes=[pltpu.VMEM((3, side_y + 2, side_x, width), F32)],
         cost_estimate=pl.CostEstimate(
             flops=54 * depth * rows * width, bytes_accessed=30 << 20, transcendentals=0
@@ -112,56 +132,75 @@
 GROUP = 16
 
 
-def scatter_kernel(rows_ref, clash_ref, base_ref, recv_ref, out_ref, acc, wide, feat, sems, base_sem):
+def scatter_kernel(
+    rows_ref, clash_ref, base_ref, recv_ref, out_ref, acc0, acc1, wide, feat, feat_sems, base_sems
+):
     slots, block_rows = rows_ref.shape
-    total, width = acc.shape
+    total = acc0.shape[0]
+    accs = (acc0, acc1)
+    pieces = feat_sems.shape[0]
+    each = slots // pieces
     step = 1024
 
-    base_copy = pltpu.make_async_copy(base_ref, acc, base_sem)
-    base_copy.start()
-
-    def fetch(j):
+    def base_copy(h):
+        return pltpu.make_async_copy(base_ref.at[h], accs[h], base_sems.at[h])
+
+    def fetch(i):
         return pltpu.make_async_copy(
-            recv_ref.at[j, pl.ds(0, block_rows)], feat.at[lax.rem(j, 4)], sems.at[lax.rem(j, 4)]
-        )
-
-    for j in range(3):
-        fetch(j).start()
-    base_copy.wait()
+            recv_ref.at[pl.ds(i * each, each), pl.ds(0, block_rows)],
+            feat.at[pl.ds(i * each, each)],
+            feat_sems.at[i],
+        )
+
+    for h in range(2):
+        base_copy(h).start()
+    for i in range(pieces):
+        fetch(i).start()
+    for h in range(2):
+        base_copy(h).wait()
+
+    def add_row(j, c, offset):
+        r = rows_ref[j, c]
+        for h in range(2):
+            accs[h][pl.ds(r, 1), :] = (
+                accs[h][pl.ds(r, 1), :] + wide[h, pl.ds(offset, 1), :]
+            )
 
     def one(j, carry):
-        fetch(j).wait()
-
-        @pl.when(j + 3 < slots)
+        @pl.when(lax.rem(j, each) == 0)
         def _():
-            fetch(j + 3).start()
+            fetch(j // each).wait()
 
         @pl.when(rows_ref[j, 0] < total)
         def _():
-            wide[...] = feat[lax.rem(j, 4)].astype(F32)
-
-            def group(g, inner):
+            for h in range(2):
+                wide[h] = feat[j, :, pl.ds(128 * h, 128)].astype(F32)
+
+            for g in range(block_rows // GROUP):
                 first = g * GROUP
-                where = [rows_ref[j, first + k] for k in range(GROUP)]
-                base = pl.multiple_of(first, GROUP)
 
                 @pl.when(clash_ref[j, g] == 0)
                 def _():
-                    olds = [acc[pl.ds(r, 1), :] for r in where]
+                    where = [rows_ref[j, first + k] for k in range(GROUP)]
                     news = [
-                        old + wide[pl.ds(base + k, 1), :] for k, old in enumerate(olds)
+                        [
+                            accs[h][pl.ds(r, 1), :]
+                            + wide[h, first + k : first + k + 1, :]
+                            for h in range(2)
+                        ]
+                        for k, r in enumerate(where)
                     ]
                     for r, new in zip(where, news):
-                        acc[pl.ds(r, 1), :] = new
+                        for h in range(2):
+                            accs[h][pl.ds(r, 1), :] = new[h]
 
                 @pl.when(clash_ref[j, g] != 0)
                 def _():
-                    for k, r in enumerate(where):
-                        acc[pl.ds(r, 1), :] = acc[pl.ds(r, 1), :] + wide[pl.ds(base + k, 1), :]
-
-                return inner
-
-            lax.fori_loop(0, block_rows // GROUP, group, 0)
+                    def single(k, inner):
+                        add_row(j, first + k, first + k)
+                        return inner
+
+                    lax.fori_loop(0, GROUP, single, 0)
 
         return carry
 
@@ -169,15 +208,17 @@
 
     def finish(i, carry):
         part = pl.ds(pl.multiple_of(i * step, step), step)
-        out_ref[part, :] = acc[part, :].astype(BF16)
+        for h in range(2):
+            out_ref[part, pl.ds(128 * h, 128)] = accs[h][part, :].astype(BF16)
         return carry
 
     lax.fori_loop(0, total // step, finish, 0)
 
 
 def scatter(rows, clash, base, recv):
-    total, width = base.shape
-    block_rows = rows.shape[1]
+    _, total, lanes = base.shape
+    slots, block_rows = rows.shape
+    width = 2 * lanes
     return pl.pallas_call(
         scatter_kernel,
         out_shape=jax.ShapeDtypeStruct((total, width), BF16),
@@ -189,11 +230,12 @@
         ],
         out_specs=whole(),
         scratch_shapes=[
-            pltpu.VMEM((total, width), F32),
-            pltpu.VMEM((block_rows, width), F32),
-            pltpu.VMEM((4, block_rows, width), BF16),
-            pltpu.SemaphoreType.DMA((4,)),
-            pltpu.SemaphoreType.DMA,
+            pltpu.VMEM((total, lanes), F32),
+            pltpu.VMEM((total, lanes), F32),
+            pltpu.VMEM((2, block_rows, lanes), F32),
+            pltpu.VMEM((slots, block_rows, width), BF16),
+            pltpu.SemaphoreType.DMA((8,)),
+            pltpu.SemaphoreType.DMA((2,)),
         ],
         cost_estimate=pl.CostEstimate(flops=2 << 20, bytes_accessed=16 << 20, transcendentals=0),
         name="scatter",
@@ -251,7 +293,8 @@
     quarter = xbuf.shape[1]
     size = quarter // CHUNKS
     width = xbuf.shape[2]
-    count = slabs - 1
+    half = slabs // 2
+    z_hi, spot = slab // half, slab % half
 
     def local_copies():
         yield pltpu.make_async_copy(
@@ -264,8 +307,8 @@
 
     barrier = pltpu.get_barrier_semaphore()
     for d in (1, 2, 3):
-        pl.semaphore_signal(barrier, inc=1, device_id=(slab, peers[d]), device_id_type=MESH)
-    pl.semaphore_signal(barrier, inc=1, device_id=(far_slab, peers[2]), device_id_type=MESH)
+        for where in (slab, far_slab):
+            pl.semaphore_signal(barrier, inc=1, device_id=(where, peers[d]), device_id_type=MESH)
 
     def greet(k, carry):
         pl.semaphore_signal(
@@ -274,7 +317,7 @@
         return carry
 
     lax.fori_loop(1, slabs, greet, 0)
-    pl.semaphore_wait(barrier, 4 + count)
+    pl.semaphore_wait(barrier, 6 + slabs - 1)
 
     def x_copy(d, i):
         rows = pl.ds(i * size, size)
@@ -302,13 +345,12 @@
             device_id_type=MESH,
         )
 
-    def a_copy(d, i):
-        rows = pl.ds(chan * quarter + i * size, size)
+    def a_copy(d):
         return pltpu.make_async_remote_copy(
-            src_ref=own.at[pl.ds(i * size, size)],
-            dst_ref=assign_ref.at[rows],
-            send_sem=a_send.at[d - 1, i],
-            recv_sem=a_recv.at[d - 1, i],
+            src_ref=own,
+            dst_ref=assign_ref.at[pl.ds(chan * quarter, quarter)],
+            send_sem=a_send.at[d - 1],
+            recv_sem=a_recv.at[d - 1],
             device_id=(slab, peers[d]),
             device_id_type=MESH,
         )
@@ -343,15 +385,12 @@
         top = jnp.max(scores, axis=1, keepdims=True)
         power = jnp.exp(scores - top)
         own[rows, :] = (power / jnp.sum(power, axis=1, keepdims=True)).astype(BF16)
-        for d in (1, 2):
-            a_copy(d, i).start()
 
     def pool_chunk(i):
         rows = pl.ds(pl.multiple_of(i * size, size), size)
         assign = own[rows, :]
-        ones = jnp.ones((size, 128), BF16)
         over_rows = (((0,), (0,)), ((), ()))
-        totals[...] += lax.dot_general(assign, ones, over_rows, preferred_element_type=F32)
+        totals[...] += jnp.dot(jnp.ones((16, size), BF16), assign, preferred_element_type=F32)
         for p in range(4):
             both = jnp.dot(nbuf[rows, :], wbuf[p], preferred_element_type=F32)
             gated = (both[:, :width] * jax.nn.sigmoid(both[:, width:])).astype(BF16)
@@ -373,47 +412,58 @@
         pool_chunk(2 * i + 1)
         return carry
 
-    lax.fori_loop(0, CHUNKS // 2, late, 0)
-
+    lax.fori_loop(0, CHUNKS // 2 - 1, late, 0)
+    pool_chunk(CHUNKS - 2)
+    assign_chunk(CHUNKS - 1)
+    pool_chunk(CHUNKS - 1)
+
+    column = [(far, d) for far in range(2) for d in range(4)][1:]
+    held = pooled.shape[1] // 2
+
+    def p_copy(n):
+        far, d = column[n]
+        return pltpu.make_async_remote_copy(
+            src_ref=part_out.at[(z_hi + far) % 2, peers[d]],
+            dst_ref=part_in.at[n],
+            send_sem=p_send.at[n],
+            recv_sem=p_recv.at[n],
+            device_id=((slab + far * half) % slabs, peers[d]),
+            device_id_type=MESH,
+        )
+
+    weights = totals[...]
+    for p in range(4):
+        for h in range(2):
+            part_out[h, p, pl.ds(0, held)] = pooled[p, pl.ds(h * held, held)].astype(BF16)
+            part_out[h, p, pl.ds(held, 16), pl.ds(0, 128)] = weights.astype(BF16)
+            part_out[h, p, pl.ds(held, 16), pl.ds(128, width - 128)] = jnp.zeros(
+                (16, width - 128), BF16
+            )
+    for n in (1, 2, 3, 4, 5, 6, 0):
+        p_copy(n).start()
+    for d in (2, 1):
+        a_copy(d).start()
     keep = pltpu.make_async_copy(own, assign_ref.at[pl.ds(chan * quarter, quarter)], local_sem.at[0])
     keep.start()
-
-    def p_copy(d):
-        return pltpu.make_async_remote_copy(
-            src_ref=part_out.at[peers[d]],
-            dst_ref=part_in.at[d - 1],
-            send_sem=p_send.at[d - 1],
-            recv_sem=p_recv.at[d - 1],
-            device_id=(slab, peers[d]),
-            device_id_type=MESH,
-        )
-
-    for p in range(4):
-        part_out[p, :, pl.ds(0, width)] = pooled[p].astype(BF16)
-        part_out[p, :, pl.ds(width, 128)] = totals[...].astype(BF16)
-    for d in (2, 3, 1):
-        p_copy(d).start()
-    for d in (1, 2, 3):
-        p_copy(d).wait_recv()
-    mine = pooled[chan]
-    weight = totals[...]
-    for d in range(3):
-        mine = mine + part_in[d, :, pl.ds(0, width)].astype(F32)
-        weight = weight + part_in[d, :, pl.ds(width, 128)].astype(F32)
-
-    for t in range(slabs):
-        tile = (slice(8 * (t // 2), 8 * (t // 2) + 8), slice(128 * (t % 2), 128 * (t % 2) + 128))
-        tile_out[t, 0] = mine[tile]
-        tile_out[t, 1] = weight[tile[0]]
+    for n in range(7):
+        p_copy(n).wait_recv()
+    mine = pooled[chan, pl.ds(pl.multiple_of(z_hi * held, held), held)]
+    for n in range(7):
+        mine = mine + part_in[n, pl.ds(0, held)].astype(F32)
+        weights = weights + part_in[n, pl.ds(held, 16), pl.ds(0, 128)].astype(F32)
+
+    for t in range(half):
+        tile_out[t, 0] = mine[8 * (t // 2) : 8 * (t // 2) + 8, 128 * (t % 2) : 128 * (t % 2) + 128]
+        tile_out[t, 1] = weights[:8]
 
     def t_copy(k):
-        to = (slab + k) % slabs
+        to = (spot + k) % half
         return pltpu.make_async_remote_copy(
             src_ref=tile_out.at[to],
-            dst_ref=tile_in.at[slab],
+            dst_ref=tile_in.at[spot],
             send_sem=t_send.at[k - 1],
             recv_sem=t_recv.at[k - 1],
-            device_id=(to, chan),
+            device_id=(z_hi * half + to, chan),
             device_id_type=MESH,
         )
 
@@ -427,23 +477,27 @@
             device_id_type=MESH,
         )
 
-    def over_peers(action):
+    def over(number, action):
         def body(k, carry):
             action(k)
             return carry
 
-        lax.fori_loop(1, slabs, body, 0)
-
-    over_peers(lambda k: t_copy(k).start())
-    tile_in[slab] = tile_out[slab]
-    over_peers(lambda k: t_copy(k).wait_recv())
+        lax.fori_loop(1, number, body, 0)
+
+    over(half, lambda k: t_copy(k).start())
+    tile_in[spot] = tile_out[spot]
+    over(half, lambda k: t_copy(k).wait_recv())
     sums = jnp.sum(tile_in[...], axis=0)
-    held = latents_ref[
-        pl.ds(pl.multiple_of(8 * (slab // 2), 8), 8), pl.ds(pl.multiple_of(128 * (slab % 2), 128), 128)
+    first = z_hi * held + 8 * (spot // 2)
+    row = lax.broadcasted_iota(jnp.int32, (8, 128), 0)
+    lane = lax.broadcasted_iota(jnp.int32, (8, 128), 1)
+    weight = jnp.sum(jnp.where(lane == row + first, sums[1], 0.0), axis=1, keepdims=True)
+    before = latents_ref[
+        pl.ds(pl.multiple_of(first, 8), 8), pl.ds(pl.multiple_of(128 * (spot % 2), 128), 128)
     ]
-    fresh = held + sums[0] / (sums[1] + 1.0)
+    fresh = before + sums[0] / (weight + 1.0)
     new_out[...] = fresh
-    over_peers(lambda k: n_copy(k).start())
+    over(slabs, lambda k: n_copy(k).start())
     new_in[slab] = fresh
 
     def forward():
@@ -451,27 +505,21 @@
         return pltpu.make_async_remote_copy(
             src_ref=assign_ref.at[rows],
             dst_ref=assign_ref.at[rows],
-            send_sem=a_send.at[2, 0],
-            recv_sem=a_recv.at[2, 0],
+            send_sem=a_send.at[2],
+            recv_sem=a_recv.at[2],
             device_id=(slab, peers[1]),
             device_id_type=MESH,
         )
 
-    def landed(i, carry):
-        a_copy(2, i).wait_recv()
-        return carry
-
-    lax.fori_loop(0, CHUNKS, landed, 0)
+    a_copy(2).wait_recv()
     forward().start()
 
-    over_peers(lambda k: n_copy(k).wait_recv())
+    over(slabs, lambda k: n_copy(k).wait_recv())
     for t in range(slabs):
-        latent_ref[8 * (t // 2) : 8 * (t // 2) + 8, 128 * (t % 2) : 128 * (t % 2) + 128] = new_in[t]
+        top, left = held * (t // half) + 8 * ((t % half) // 2), 128 * (t % 2)
+        latent_ref[top : top + 8, left : left + 128] = new_in[t]
 
     def drained(i, carry):
-        a_copy(1, i).wait_recv()
-        for d in (1, 2):
-            a_copy(d, i).wait_send()
         for d in (1, 2, 3):
             x_copy(d, i).wait_send()
         return carry
@@ -479,10 +527,13 @@
     lax.fori_loop(0, CHUNKS, drained, 0)
     for which in range(3):
         w_copy(which).wait_send()
-    for d in (1, 2, 3):
-        p_copy(d).wait_send()
-    over_peers(lambda k: t_copy(k).wait_send())
-    over_peers(lambda k: n_copy(k).wait_send())
+    for n in range(7):
+        p_copy(n).wait_send()
+    over(half, lambda k: t_copy(k).wait_send())
+    over(slabs, lambda k: n_copy(k).wait_send())
+    a_copy(1).wait_recv()
+    for d in (1, 2):
+        a_copy(d).wait_send()
     forward().wait()
     keep.wait()
 
@@ -513,11 +564,11 @@
             pltpu.VMEM((4,) + weights.shape, BF16),
             pltpu.VMEM((quarter, held), BF16),
             pltpu.VMEM((4, held, width), F32),
-            pltpu.VMEM((held, 128), F32),
-            pltpu.VMEM((4, held, width + 128), BF16),
-            pltpu.VMEM((3, held, width + 128), BF16),
-            pltpu.VMEM((slabs, 2, 8, 128), F32),
-            pltpu.VMEM((slabs, 2, 8, 128), F32),
+            pltpu.VMEM((16, 128), F32),
+            pltpu.VMEM((2, 4, held // 2 + 16, width), BF16),
+            pltpu.VMEM((7, held // 2 + 16, width), BF16),
+            pltpu.VMEM((slabs // 2, 2, 8, 128), F32),
+            pltpu.VMEM((slabs // 2, 2, 8, 128), F32),
             pltpu.VMEM((8, 128), F32),
             pltpu.VMEM((slabs, 8, 128), F32),
             dma((2,)),
@@ -525,12 +576,12 @@
             dma((3, CHUNKS)),
             dma((3,)),
             dma((3,)),
-            dma((3, CHUNKS)),
-            dma((3, CHUNKS)),
             dma((3,)),
             dma((3,)),
-            dma((slabs - 1,)),
-            dma((slabs - 1,)),
+            dma((7,)),
+            dma((7,)),
+            dma((slabs // 2 - 1,)),
+            dma((slabs // 2 - 1,)),
             dma((slabs - 1,)),
             dma((slabs - 1,)),
         ],
@@ -561,23 +612,12 @@
     capacity = max(2, (2 * blocks + slabs - 1) // slabs)
     slots = slabs * capacity
 
-    targets = refine_dest[:, 0]
-    ids = jnp.arange(blocks, dtype=jnp.int32)
-    earlier = (targets[None, :] == targets[:, None]) & (ids[None, :] < ids[:, None])
-    position = targets * capacity + jnp.sum(earlier.astype(jnp.int32), axis=1)
-    chosen = position[None, :] == jnp.arange(slots, dtype=jnp.int32)[:, None]
-    source = jnp.sum(jnp.where(chosen, ids[None, :], 0), axis=1)
-    filled = jnp.any(chosen, axis=1)
-    wanted = jnp.where(filled[:, None], refine_rows[source], row_count)
-    code = jnp.concatenate([wanted // 128, wanted % 128], axis=1).astype(BF16)
-    code = jnp.broadcast_to(code[:, None, :], (slots, EXTRA, width))
-
     up = [(i, i + 1) for i in range(slabs - 1)]
     down = [(i + 1, i) for i in range(slabs - 1)]
     before = lax.ppermute(tokens[-1:], "slab", up)
     after = lax.ppermute(tokens[:1], "slab", down)
 
-    sent = pack(source, refine_feat, code)
+    sent = pack(refine_dest[:, 0], refine_feat, refine_rows, slabs, capacity, row_count)
     sent, before, after = lax.optimization_barrier((sent, before, after))
     received = lax.all_to_all(
         sent.reshape(slabs, capacity * (block_rows + EXTRA), width),

time: 251 us -> 211 us (0.84)
  Pallas kernels: 183 us -> 145 us
  waiting for transfers between devices: 34.8 us -> 37.6 us
    pallas_call x1, Pallas kernels: 70.3 us -> 20.7 us  [scatter(): pl.pallas_call(scatter_kernel, out_shape=jax.ShapeDtypeStruct((total, wid...]
    pallas_call x1, Pallas kernels: 82.2 us -> 93 us  [mix(): pl.pallas_call(mix_kernel, out_shape=(jax.ShapeDtypeStruct((rows, held),...]
    ppermute x1, waiting for transfers between devices: 2.36 us -> 5.31 us  [per_device(): before = lax.ppermute(tokens[-1:], 'slab', up)]
  transfers between devices with their start and end apart: 3 -> 3, of which waited for: 3 -> 3; matrix products, arithmetic and copies ran while one was open for 1% -> 0% of each run, Pallas kernels for 12% -> 15%
where the time goes in v2:
time: 211 us
  Pallas kernels  145 us (69%)
  waiting for transfers between devices  37.6 us (18%)
  starting transfers between devices  19.5 us (9%)
  local copies, waits for them, and re-layouts  3.53 us (2%)
  matrix products  3.25 us (2%)
    pallas_call x1, Pallas kernels, mix(): pl.pallas_call(mix_kernel, out_shape=(jax.ShapeDtypeStruct((rows, held),...  93 us
    all_to_all x1, waiting for transfers between devices, per_device(): lax.all_to_all(sent.reshape(slabs, capacity * (block_rows + EXTRA), width...  28.1 us
    pallas_call x1, Pallas kernels, conv(): pl.pallas_call(conv_kernel, grid=(depth,), out_shape=jax.ShapeDtypeStruct...  26.5 us
    pallas_call x1, Pallas kernels, scatter(): pl.pallas_call(scatter_kernel, out_shape=jax.ShapeDtypeStruct((total, wid...  20.7 us
    all_to_all x1, starting transfers between devices, per_device(): lax.all_to_all(sent.reshape(slabs, capacity * (block_rows + EXTRA), width...  14.6 us
    ppermute x1, waiting for transfers between devices, per_device(): before = lax.ppermute(tokens[-1:], 'slab', up)  5.31 us
    pallas_call x1, Pallas kernels, pack(): pl.pallas_call(functools.partial(pack_kernel, capacity, empty), out_shape...  4.52 us
  transfers between devices with their start and end apart: 3, of which 3 were waited for; matrix products, arithmetic and copies ran while one was open for 0% of the time, Pallas kernels for 15%

profile of v2, /device:TPU:0, one launch (start us, length us, event | category | flops | bytes accessed | tf_op | source)
XLA Modules:
  0.0 210.6 jit_solution(6113974284686722892)
XLA Ops:
  0.6 1.3 fusion.2
  1.9 3.6 %collective-permute-start = (bf16[1,32,32,256]{3,2,1,0:T(8,128)(2,1)S(1)}, bf16[1,32,32,256]{3,2,1,0:T(8,128)(2,1)S(1)}, u32[]{:S(2)}, u32[]{:S(2)}) collective-permute-start(bf16[1,32,32,256]{3,2,1,0:T(8,128)(2,1)S(1)} %get-tuple-element.13), channel_id=1, source_target_pairs={{0,4},{4,8},{8,12},{12,16},{16,20},{20,24},{24,28},{28,32},{32,36}... | collective-permute-start | bytes 1572872 | tf_op jit(solution)/shard_map/ppermute | solution.py:617
  5.5 1.3 collective-permute-start.1
  6.8 4.5 %pack.1 = bf16[64,136,256]{2,1,0:T(8,128)(2,1)} custom-call(s32[32]{0:T(128)} %bitcast.15, bf16[32,128,256]{2,1,0:T(8,128)(2,1)} %feat_ref.1, s32[32,128]{1,0:T(8,128)} %rows_ref.1), custom_call_target="tpu_custom_call" | custom-call | bytes 6291456 | tf_op jit(solution)/shard_map/pack/pallas_call | solution.py:53
  11.4 5.3 %collective-permute-done.before_ref = bf16[1,32,32,256]{3,2,1,0:T(8,128)(2,1)S(1)} collective-permute-done((bf16[1,32,32,256]{3,2,1,0:T(8,128)(2,1)S(1)}, bf16[1,32,32,256]{3,2,1,0:T(8,128)(2,1)S(1)}, u32[]{:S(2)}, u32[]{:S(2)}) %collective-permute-start) | collective-permute-done | bytes 524320 | tf_op jit(solution)/shard_map/ppermute | solution.py:617
  16.7 4.1 %collective-permute-done.1.after_ref = bf16[1,32,32,256]{3,2,1,0:T(8,128)(2,1)S(1)} collective-permute-done((bf16[1,32,32,256]{3,2,1,0:T(8,128)(2,1)S(1)}, bf16[1,32,32,256]{3,2,1,0:T(8,128)(2,1)S(1)}, u32[]{:S(2)}, u32[]{:S(2)}) %collective-permute-start.1) | collective-permute-done | bytes 524320 | tf_op jit(solution)/shard_map/ppermute | solution.py:618
  20.8 0.8 copy-done.7
  21.6 14.6 %all-to-all-start = ((bf16[32,272,256]{2,1,0:T(8,128)(2,1)}), bf16[32,272,256]{2,1,0:T(8,128)(2,1)}, u32[]{:S(2)}, u32[]{:S(2)}) async-start(bf16[32,272,256]{2,1,0:T(8,128)(2,1)} %bitcast.11), calls=%async_computation | async-start | bytes 8912896 | tf_op jit(solution)/shard_map/all_to_all | solution.py:622
  36.2 0.0 copy-done.4
  36.2 0.0 copy-done.5
  36.2 0.1 pad_maximum_fusion.w_ref
  36.3 26.5 %conv.1.base_ref = f32[2,8192,128]{2,1,0:T(8,128)} custom-call(bf16[8,32,32,256]{3,2,1,0:T(8,128)(2,1)} %tokens_ref.1, bf16[1,32,32,256]{3,2,1,0:T(8,128)(2,1)} %copy-done.6, bf16[1,32,32,256]{3,2,1,0:T(8,128)(2,1)} %copy-done.7, f32[27,256]{1,0:T(8,128)} %w_ref.1), custom_call_target="tpu_custom_call" | custom-call | flops 113246208 | bytes 31457280 | tf_op jit(solution)/shard_map/conv/pallas_call | solution.py:118
  62.8 28.1 %all-to-all-done = bf16[32,272,256]{2,1,0:T(8,128)(2,1)} async-done(((bf16[32,272,256]{2,1,0:T(8,128)(2,1)}), bf16[32,272,256]{2,1,0:T(8,128)(2,1)}, u32[]{:S(2)}, u32[]{:S(2)}) %all-to-all-start) | async-done | bytes 4456480 | tf_op jit(solution)/shard_map/all_to_all | solution.py:622
  90.9 1.0 slice_convert_fusion
  92.0 0.0 copy-start.8
  92.0 0.1 copy.17
  92.1 0.2 and_reduce_fusion
  92.3 0.7 copy.18.clash_ref
  93.0 0.0 copy-done.8
  93.0 20.7 %scatter.1.mixed_ref = bf16[8192,256]{1,0:T(8,128)(2,1)} custom-call(s32[64,128]{1,0:T(8,128)} %copy-done.8, s32[64,8]{1,0:T(8,128)} %copy.18.clash_ref, f32[2,8192,128]{2,1,0:T(8,128)} %conv.1.base_ref, bf16[64,136,256]{2,1,0:T(8,128)(2,1)} %bitcast.2.recv_ref), custom_call_target="tpu_custom_call" | custom-call | flops 2097152 | bytes 16777216 | tf_op jit(solution)/shard_map/scatter/pallas_call | solution.py:222
  113.7 0.0 copy-start.3
  113.7 93.0 %mix.1 = (bf16[8192,128]{1,0:T(8,128)(2,1)S(1)}, f32[128,256]{1,0:T(8,128)S(1)}) custom-call(bf16[8192,256]{1,0:T(8,128)(2,1)} %scatter.1.mixed_ref, bf16[1024,512]{1,0:T(8,128)(2,1)S(1)} %pad_maximum_fusion.w_ref, bf16[128,1024]{1,0:T(8,128)(2,1)S(1)} %copy-done, f32[1,1024]{1,0:T(1,128)S(1)} %bitcast.10, f32[128,256]{1,0:T(8,128)S(1)} %copy-done.1), custom_call_target="tpu_custom_call" | custom-call | flops 10737418240 | bytes 16777216 | tf_op jit(solution)/shard_map/mix/pallas_call | solution.py:547
  206.7 3.3 %fusion = bf16[8192,256]{1,0:T(8,128)(2,1)} fusion(bf16[8192,128]{1,0:T(8,128)(2,1)S(1)} %get-tuple-element.10, bf16[8192,256]{1,0:T(8,128)(2,1)S(1)} %copy-done.3, f32[128,256]{1,0:T(8,128)S(1)} %get-tuple-element.17), kind=kOutput, calls=%fused_computation.1 | convolution fusion | flops 543195136 | bytes 10616832 | tf_op jit(solution)/shard_map/dot_general | solution.py:642
  209.9 0.7 copy.23
  (16 shorter events, 0.0 us)
Async XLA Ops:
  1.9 14.8 %collective-permute-start = (bf16[1,32,32,256]{3,2,1,0:T(8,128)(2,1)S(1)}, bf16[1,32,32,256]{3,2,1,0:T(8,128)(2,1)S(1)}, u32[]{:S(2)}, u32[]{:S(2)}) collective-permute-start(bf16[1,32,32,256]{3,2,1,0:T(8,128)(2,1)S(1)} %get-tuple-element.13), channel_id=1, source_target_pairs={{0,4},{4,8},{8,12},{12,16},{16,20},{20,24},{24,28},{28,32},{32,36}... | collective-permute-start | bytes 1572872 | tf_op jit(solution)/shard_map/ppermute | solution.py:617
  5.5 15.3 %collective-permute-start.1 = (bf16[1,32,32,256]{3,2,1,0:T(8,128)(2,1)S(1)}, bf16[1,32,32,256]{3,2,1,0:T(8,128)(2,1)S(1)}, u32[]{:S(2)}, u32[]{:S(2)}) collective-permute-start(bf16[1,32,32,256]{3,2,1,0:T(8,128)(2,1)S(1)} %get-tuple-element.12), channel_id=1, source_target_pairs={{4,0},{8,4},{12,8},{16,12},{20,16},{24,20},{28,24},{32,28},{36,32}... | collective-permute-start | bytes 1572872 | tf_op jit(solution)/shard_map/ppermute | solution.py:618
  16.7 4.2 %copy-start.6 = (bf16[1,32,32,256]{3,2,1,0:T(8,128)(2,1)}, bf16[1,32,32,256]{3,2,1,0:T(8,128)(2,1)S(1)}, u32[]{:S(2)}) copy-start(bf16[1,32,32,256]{3,2,1,0:T(8,128)(2,1)S(1)} %collective-permute-done.before_ref) | copy-start | bytes 1572868
  20.8 0.8 copy-start.7
  20.8 15.4 %copy-start.4 = (bf16[1024,256]{1,0:T(8,128)(2,1)S(1)}, bf16[1024,256]{1,0:T(8,128)(2,1)}, u32[]{:S(2)}) copy-start(bf16[1024,256]{1,0:T(8,128)(2,1)} %param.17) | copy-start | bytes 1572868
  20.8 15.4 %copy-start.5 = (bf16[1024,256]{1,0:T(8,128)(2,1)S(1)}, bf16[1024,256]{1,0:T(8,128)(2,1)}, u32[]{:S(2)}) copy-start(bf16[1024,256]{1,0:T(8,128)(2,1)} %param.16) | copy-start | bytes 1572868
  21.6 69.3 %all-to-all-start = ((bf16[32,272,256]{2,1,0:T(8,128)(2,1)}), bf16[32,272,256]{2,1,0:T(8,128)(2,1)}, u32[]{:S(2)}, u32[]{:S(2)}) async-start(bf16[32,272,256]{2,1,0:T(8,128)(2,1)} %bitcast.11), calls=%async_computation | async-start | bytes 8912896 | tf_op jit(solution)/shard_map/all_to_all | solution.py:622
  92.0 1.0 copy-start.8
  93.0 20.7 %copy-start = (bf16[128,1024]{1,0:T(8,128)(2,1)S(1)}, bf16[128,1024]{1,0:T(8,128)(2,1)}, u32[]{:S(2)}) copy-start(bf16[128,1024]{1,0:T(8,128)(2,1)} %keys_ref.1) | copy-start | bytes 786436
  93.0 20.7 %copy-start.1 = (f32[128,256]{1,0:T(8,128)S(1)}, f32[128,256]{1,0:T(8,128)}, u32[]{:S(2)}) copy-start(f32[128,256]{1,0:T(8,128)} %latents_ref.1) | copy-start | bytes 393220
  93.0 20.7 %copy-start.2 = (f32[1024]{0:T(1024)S(1)}, f32[1024]{0:T(1024)}, u32[]{:S(2)}) copy-start(f32[1024]{0:T(1024)} %param.15) | copy-start | bytes 12292
  113.7 93.0 %copy-start.3 = (bf16[8192,256]{1,0:T(8,128)(2,1)S(1)}, bf16[8192,256]{1,0:T(8,128)(2,1)}, u32[]{:S(2)}) copy-start(bf16[8192,256]{1,0:T(8,128)(2,1)} %scatter.1.mixed_ref) | copy-start | bytes 12582916

commit v3 on v2

--- a/solution.py
+++ b/solution.py
@@ -6,6 +6,7 @@
 from jax.experimental import pallas as pl
 from jax.experimental.pallas import tpu as pltpu
 from jax.sharding import PartitionSpec as P
+
 
 MESH = pl.DeviceIdType.MESH
 BF16 = jnp.bfloat16
@@ -64,7 +65,7 @@
 def conv_kernel(tokens_ref, before_ref, after_ref, w_ref, out_ref, plane):
     z = pl.program_id(0)
     last = pl.num_programs(0) - 1
-    depth, side_y, side_x, width = tokens_ref.shape
+    _, side_y, side_x, width = tokens_ref.shape
 
     def widen(slot, value):
         plane[slot, pl.ds(1, side_y)] = value.astype(F32)
@@ -105,7 +106,10 @@
             centre = plane[slots[1], y + 1, :, lanes] + sums[1]
             left = jnp.where(column == 0, 0.0, pltpu.roll(sums[0], 1, 0))
             right = jnp.where(column == side_x - 1, 0.0, pltpu.roll(sums[2], side_x - 1, 0))
-            out_ref[half, pl.ds(pl.multiple_of(y * side_x, side_x), side_x), :] = centre + left + right
+            value = centre + left + right
+            for i in range(0, side_x, 8):
+                to = pl.ds(pl.multiple_of(2 * side_x * y + 2 * i + 8 * half, 8), 8)
+                out_ref[to, :] = value[i : i + 8]
             return carry
 
         lax.fori_loop(0, side_y, one, 0)
@@ -118,9 +122,9 @@
     return pl.pallas_call(
         conv_kernel,
         grid=(depth,),
-        out_shape=jax.ShapeDtypeStruct((width // 128, depth * rows, 128), F32),
+        out_shape=jax.ShapeDtypeStruct((2 * depth * rows, 128), F32),
         in_specs=[fixed(tokens.shape), fixed(before.shape), fixed(after.shape), fixed(w.shape)],
-        out_specs=pl.BlockSpec((width // 128, rows, 128), lambda z: (0, z, 0)),
+        out_specs=pl.BlockSpec((2 * rows, 128), lambda z: (z, 0)),
         scratch_shapes=[pltpu.VMEM((3, side_y + 2, side_x, width), F32)],
         cost_estimate=pl.CostEstimate(
             flops=54 * depth * rows * width, bytes_accessed=30 << 20, transcendentals=0
@@ -133,17 +137,15 @@
 
 
 def scatter_kernel(
-    rows_ref, clash_ref, base_ref, recv_ref, out_ref, acc0, acc1, wide, feat, feat_sems, base_sems
+    spots_ref, clash_ref, base_ref, recv_ref, out_ref, acc, wide, feat, feat_sems, base_sem
 ):
-    slots, block_rows = rows_ref.shape
-    total = acc0.shape[0]
-    accs = (acc0, acc1)
+    slots, block_rows = spots_ref.shape
+    total = acc.shape[0] // 2
     pieces = feat_sems.shape[0]
     each = slots // pieces
-    step = 1024
-
-    def base_copy(h):
-        return pltpu.make_async_copy(base_ref.at[h], accs[h], base_sems.at[h])
+    step = 128
+
+    base_copy = pltpu.make_async_copy(base_ref, acc, base_sem)
 
     def fetch(i):
         return pltpu.make_async_copy(
@@ -152,73 +154,74 @@
             feat_sems.at[i],
         )
 
-    for h in range(2):
-        base_copy(h).start()
+    base_copy.start()
     for i in range(pieces):
         fetch(i).start()
-    for h in range(2):
-        base_copy(h).wait()
-
-    def add_row(j, c, offset):
-        r = rows_ref[j, c]
-        for h in range(2):
-            accs[h][pl.ds(r, 1), :] = (
-                accs[h][pl.ds(r, 1), :] + wide[h, pl.ds(offset, 1), :]
-            )
+    base_copy.wait()
+
+    def at(spot):
+        return pl.ds(spot, 2, stride=8)
 
     def one(j, carry):
         @pl.when(lax.rem(j, each) == 0)
         def _():
             fetch(j // each).wait()
 
-        @pl.when(rows_ref[j, 0] < total)
+        @pl.when(spots_ref[j, 0] < 2 * total)
         def _():
-            for h in range(2):
-                wide[h] = feat[j, :, pl.ds(128 * h, 128)].astype(F32)
-
-            for g in range(block_rows // GROUP):
-                first = g * GROUP
-
-                @pl.when(clash_ref[j, g] == 0)
-                def _():
-                    where = [rows_ref[j, first + k] for k in range(GROUP)]
-                    news = [
-                        [
-                            accs[h][pl.ds(r, 1), :]
-                            + wide[h, first + k : first + k + 1, :]
-                            for h in range(2)
-                        ]
-                        for k, r in enumerate(where)
-                    ]
-                    for r, new in zip(where, news):
-                        for h in range(2):
-                            accs[h][pl.ds(r, 1), :] = new[h]
-
-                @pl.when(clash_ref[j, g] != 0)
-                def _():
-                    def single(k, inner):
-                        add_row(j, first + k, first + k)
-                        return inner
-
-                    lax.fori_loop(0, GROUP, single, 0)
+            for k in range(0, block_rows, 16):
+                for h in range(2):
+                    value = feat[j, k : k + 16, 128 * h : 128 * h + 128].astype(F32)
+                    wide[2 * k + 8 * h : 2 * k + 8 * h + 8, :] = value[:8]
+                    wide[2 * k + 16 + 8 * h : 2 * k + 24 + 8 * h, :] = value[8:]
+
+            groups = block_rows // GROUP
+            mine = [2 * (c - c % 8) + c % 8 for c in range(block_rows)]
+
+            def together(g):
+                places = range(g * GROUP, (g + 1) * GROUP)
+                where = [spots_ref[j, c] for c in places]
+                news = [acc[at(r), :] + wide[at(mine[c]), :] for r, c in zip(where, places)]
+                for r, new in zip(where, news):
+                    acc[at(r), :] = new
+
+            @pl.when(clash_ref[j, groups] == 0)
+            def _():
+                for g in range(groups):
+                    together(g)
+
+            @pl.when(clash_ref[j, groups] != 0)
+            def _():
+                for g in range(groups):
+
+                    @pl.when(clash_ref[j, g] == 0)
+                    def _():
+                        together(g)
+
+                    @pl.when(clash_ref[j, g] != 0)
+                    def _():
+                        for c in range(g * GROUP, (g + 1) * GROUP):
+                            r = spots_ref[j, c]
+                            acc[at(r), :] = acc[at(r), :] + wide[at(mine[c]), :]
 
         return carry
 
     lax.fori_loop(0, slots, one, 0)
 
     def finish(i, carry):
+        value = acc[pl.ds(pl.multiple_of(i * 2 * step, 2 * step), 2 * step), :]
+        value = value.reshape(step // 8, 2, 8, 128)
         part = pl.ds(pl.multiple_of(i * step, step), step)
         for h in range(2):
-            out_ref[part, pl.ds(128 * h, 128)] = accs[h][part, :].astype(BF16)
+            out_ref[part, 128 * h : 128 * h + 128] = value[:, h].reshape(step, 128).astype(BF16)
         return carry
 
     lax.fori_loop(0, total // step, finish, 0)
 
 
-def scatter(rows, clash, base, recv):
-    _, total, lanes = base.shape
-    slots, block_rows = rows.shape
-    width = 2 * lanes
+def scatter(spots, clash, base, recv):
+    total, width = base.shape[0] // 2, 2 * base.shape[1]
+    slots, block_rows = spots.shape
     return pl.pallas_call(
         scatter_kernel,
         out_shape=jax.ShapeDtypeStruct((total, width), BF16),
@@ -230,16 +233,15 @@
         ],
         out_specs=whole(),
         scratch_shapes=[
-            pltpu.VMEM((total, lanes), F32),
-            pltpu.VMEM((total, lanes), F32),
-            pltpu.VMEM((2, block_rows, lanes), F32),
+            pltpu.VMEM((2 * total, 128), F32),
+            pltpu.VMEM((2 * block_rows, 128), F32),
             pltpu.VMEM((slots, block_rows, width), BF16),
             pltpu.SemaphoreType.DMA((8,)),
-            pltpu.SemaphoreType.DMA((2,)),
+            pltpu.SemaphoreType.DMA,
         ],
         cost_estimate=pl.CostEstimate(flops=2 << 20, bytes_accessed=16 << 20, transcendentals=0),
         name="scatter",
-    )(rows, clash, base, recv)
+    )(spots, clash, base, recv)
 
 
 CHUNKS = 8
@@ -618,14 +620,14 @@
     after = lax.ppermute(tokens[:1], "slab", down)
 
     sent = pack(refine_dest[:, 0], refine_feat, refine_rows, slabs, capacity, row_count)
-    sent, before, after = lax.optimization_barrier((sent, before, after))
     received = lax.all_to_all(
         sent.reshape(slabs, capacity * (block_rows + EXTRA), width),
         "slab",
         split_axis=0,
         concat_axis=0,
         tiled=True,
-    ).reshape(slots, block_rows + EXTRA, width)
+    )
+    received = received.reshape(slots, block_rows + EXTRA, width)
 
     base = conv(tokens, before, after, conv_w)
     weights = jnp.concatenate([w_val, w_gate], axis=1)
@@ -635,9 +637,11 @@
     grouped = rows.reshape(slots, block_rows // GROUP, GROUP)
     same = grouped[..., :, None] == grouped[..., None, :]
     above = jnp.arange(GROUP)[:, None] < jnp.arange(GROUP)[None, :]
-    clash = jnp.any(same & above, axis=(2, 3)).astype(jnp.int32)
-
-    mixed = scatter(rows, clash, base, received)
+    clash = jnp.any(same & above, axis=(2, 3))
+    clash = jnp.concatenate([clash, jnp.any(clash, axis=1, keepdims=True)], axis=1).astype(jnp.int32)
+
+    spots = (rows // 8) * 16 + rows % 8
+    mixed = scatter(spots, clash, base, received)
     assign, latent_new = mix(mixed, weights, latent_keys, norm_gain[None, :], latents)
     readback = jnp.dot(assign, latent_new.astype(BF16), preferred_element_type=F32)
     block_out = (mixed.astype(F32) + readback).astype(BF16)

time: 211 us -> 225 us (1.066)
  waiting for transfers between devices: 37.6 us -> 56.3 us
  Pallas kernels: 145 us -> 141 us
  starting transfers between devices: 19.5 us -> 15.9 us
    ppermute x1, waiting for transfers between devices: 5.31 us -> 56.3 us  [per_device(): before = lax.ppermute(tokens[-1:], 'slab', up)]
    all_to_all x1, waiting for transfers between devices: 28.1 us -> 0.01 us  [per_device(): lax.all_to_all(sent.reshape(slabs, capacity * (block_rows + EXTRA), width...]
    pallas_call x1, Pallas kernels: 20.7 us -> 15.7 us  [scatter(): pl.pallas_call(scatter_kernel, out_shape=jax.ShapeDtypeStruct((total, wid...]
    ppermute x1, waiting for transfers between devices: 4.14 us -> 0.01 us  [per_device(): after = lax.ppermute(tokens[:1], 'slab', down)]
    all_to_all x1, starting transfers between devices: 14.6 us -> 11 us  [per_device(): lax.all_to_all(sent.reshape(slabs, capacity * (block_rows + EXTRA), width...]
  transfers between devices with their start and end apart: 3 -> 3, of which waited for: 3 -> 1; matrix products, arithmetic and copies ran while one was open for 0% -> 1% of each run, Pallas kernels for 15% -> 12%
where the time goes in v3:
time: 225 us; the launch traced here: 223 us
  Pallas kernels  141 us (63%)
  waiting for transfers between devices  56.3 us (25%)
  starting transfers between devices  15.9 us (7%)
  local copies, waits for them, and re-layouts  4.33 us (2%)
  matrix products  3.25 us (1%)
    pallas_call x1, Pallas kernels, mix(): pl.pallas_call(mix_kernel, out_shape=(jax.ShapeDtypeStruct((rows, held),...  93.9 us
    ppermute x1, waiting for transfers between devices, per_device(): before = lax.ppermute(tokens[-1:], 'slab', up)  56.3 us
    pallas_call x1, Pallas kernels, conv(): pl.pallas_call(conv_kernel, grid=(depth,), out_shape=jax.ShapeDtypeStruct...  26.5 us
    pallas_call x1, Pallas kernels, scatter(): pl.pallas_call(scatter_kernel, out_shape=jax.ShapeDtypeStruct((total, wid...  15.7 us
    all_to_all x1, starting transfers between devices, per_device(): lax.all_to_all(sent.reshape(slabs, capacity * (block_rows + EXTRA), width...  11 us
    pallas_call x1, Pallas kernels, pack(): pl.pallas_call(functools.partial(pack_kernel, capacity, empty), out_shape...  4.52 us
  transfers between devices with their start and end apart: 3, of which 1 were waited for; matrix products, arithmetic and copies ran while one was open for 1% of the time, Pallas kernels for 12%

profile of v3, /device:TPU:0, one launch (start us, length us, event | category | flops | bytes accessed | tf_op | source)
XLA Modules:
  0.0 223.3 jit_solution(16470318937325631241)
XLA Ops:
  0.6 4.5 %pack.1 = bf16[64,136,256]{2,1,0:T(8,128)(2,1)} custom-call(s32[32]{0:T(128)} %bitcast.17, bf16[32,128,256]{2,1,0:T(8,128)(2,1)} %feat_ref.1, s32[32,128]{1,0:T(8,128)} %rows_ref.1), custom_call_target="tpu_custom_call" | custom-call | bytes 6291456 | tf_op jit(solution)/shard_map/pack/pallas_call | solution.py:54
  5.2 11.0 %all-to-all-start = ((bf16[32,272,256]{2,1,0:T(8,128)(2,1)}), bf16[32,272,256]{2,1,0:T(8,128)(2,1)}, u32[]{:S(2)}, u32[]{:S(2)}) async-start(bf16[32,272,256]{2,1,0:T(8,128)(2,1)} %bitcast.12), calls=%async_computation | async-start | bytes 8912896 | tf_op jit(solution)/shard_map/all_to_all | solution.py:623
  16.1 1.3 fusion.12
  17.4 3.7 %collective-permute-start = (bf16[1,32,32,256]{3,2,1,0:T(8,128)(2,1)S(1)}, bf16[1,32,32,256]{3,2,1,0:T(8,128)(2,1)S(1)}, u32[]{:S(2)}, u32[]{:S(2)}) collective-permute-start(bf16[1,32,32,256]{3,2,1,0:T(8,128)(2,1)S(1)} %get-tuple-element.11), channel_id=1, source_target_pairs={{0,4},{4,8},{8,12},{12,16},{16,20},{20,24},{24,28},{28,32},{32,36}... | collective-permute-start | bytes 1572872 | tf_op jit(solution)/shard_map/ppermute | solution.py:619
  21.1 1.3 collective-permute-start.1
  22.4 0.0 copy-done.4
  22.4 0.0 copy-done.5
  22.4 0.1 pad_maximum_fusion.w_ref
  22.5 56.3 %collective-permute-done.before_ref = bf16[1,32,32,256]{3,2,1,0:T(8,128)(2,1)S(1)} collective-permute-done((bf16[1,32,32,256]{3,2,1,0:T(8,128)(2,1)S(1)}, bf16[1,32,32,256]{3,2,1,0:T(8,128)(2,1)S(1)}, u32[]{:S(2)}, u32[]{:S(2)}) %collective-permute-start) | collective-permute-done | bytes 524320 | tf_op jit(solution)/shard_map/ppermute | solution.py:619
  78.8 0.0 collective-permute-done.1.after_ref
  78.8 0.8 copy-done.6
  79.6 0.8 copy-done.7
  80.3 26.5 %conv.1.base_ref = f32[16384,128]{1,0:T(8,128)} custom-call(bf16[8,32,32,256]{3,2,1,0:T(8,128)(2,1)} %tokens_ref.1, bf16[1,32,32,256]{3,2,1,0:T(8,128)(2,1)} %copy-done.6, bf16[1,32,32,256]{3,2,1,0:T(8,128)(2,1)} %copy-done.7, f32[27,256]{1,0:T(8,128)} %w_ref.1), custom_call_target="tpu_custom_call" | custom-call | flops 113246208 | bytes 31457280 | tf_op jit(solution)/shard_map/conv/pallas_call | solution.py:122
  106.8 0.0 all-to-all-done
  106.8 1.0 slice_convert_fusion
  107.8 0.7 fusion.7
  108.5 0.1 copy.23
  108.6 0.4 fusion.1
  109.0 0.7 copy.24.clash_ref
  109.7 15.7 %scatter.1.mixed_ref = bf16[8192,256]{1,0:T(8,128)(2,1)} custom-call(s32[64,128]{1,0:T(8,128)} %get-tuple-element.8.spots_ref, s32[64,9]{1,0:T(8,128)} %copy.24.clash_ref, f32[16384,128]{1,0:T(8,128)} %conv.1.base_ref, bf16[64,136,256]{2,1,0:T(8,128)(2,1)} %bitcast.2.recv_ref), custom_call_target="tpu_custom_call" | custom-call | flops 2097152 | bytes 16777216 | tf_op jit(solution)/shard_map/scatter/pallas_call | solution.py:225
  125.4 0.0 copy-start.3
  125.4 93.9 %mix.1 = (bf16[8192,128]{1,0:T(8,128)(2,1)S(1)}, f32[128,256]{1,0:T(8,128)S(1)}) custom-call(bf16[8192,256]{1,0:T(8,128)(2,1)} %scatter.1.mixed_ref, bf16[1024,512]{1,0:T(8,128)(2,1)S(1)} %pad_maximum_fusion.w_ref, bf16[128,1024]{1,0:T(8,128)(2,1)S(1)} %copy-done, f32[1,1024]{1,0:T(1,128)S(1)} %bitcast.11, f32[128,256]{1,0:T(8,128)S(1)} %copy-done.1), custom_call_target="tpu_custom_call" | custom-call | flops 10737418240 | bytes 16777216 | tf_op jit(solution)/shard_map/mix/pallas_call | solution.py:549
  219.4 3.2 %add_convert_fusion = bf16[8192,256]{1,0:T(8,128)(2,1)} fusion(bf16[8192,256]{1,0:T(8,128)(2,1)S(1)} %copy-done.3, bf16[8192,128]{1,0:T(8,128)(2,1)S(1)} %get-tuple-element.4, f32[128,256]{1,0:T(8,128)S(1)} %get-tuple-element.15), kind=kOutput, calls=%fused_computation | convolution fusion | flops 543195136 | bytes 10616832 | tf_op jit(solution)/shard_map/dot_general | solution.py:646
  222.6 0.7 copy.29
  (14 shorter events, 0.0 us)
Async XLA Ops:
  5.1 17.3 %copy-start.4 = (bf16[1024,256]{1,0:T(8,128)(2,1)S(1)}, bf16[1024,256]{1,0:T(8,128)(2,1)}, u32[]{:S(2)}) copy-start(bf16[1024,256]{1,0:T(8,128)(2,1)} %param.17) | copy-start | bytes 1572868
  5.1 17.3 %copy-start.5 = (bf16[1024,256]{1,0:T(8,128)(2,1)S(1)}, bf16[1024,256]{1,0:T(8,128)(2,1)}, u32[]{:S(2)}) copy-start(bf16[1024,256]{1,0:T(8,128)(2,1)} %param.16) | copy-start | bytes 1572868
  5.2 101.7 %all-to-all-start = ((bf16[32,272,256]{2,1,0:T(8,128)(2,1)}), bf16[32,272,256]{2,1,0:T(8,128)(2,1)}, u32[]{:S(2)}, u32[]{:S(2)}) async-start(bf16[32,272,256]{2,1,0:T(8,128)(2,1)} %bitcast.12), calls=%async_computation | async-start | bytes 8912896 | tf_op jit(solution)/shard_map/all_to_all | solution.py:623
  17.4 61.3 %collective-permute-start = (bf16[1,32,32,256]{3,2,1,0:T(8,128)(2,1)S(1)}, bf16[1,32,32,256]{3,2,1,0:T(8,128)(2,1)S(1)}, u32[]{:S(2)}, u32[]{:S(2)}) collective-permute-start(bf16[1,32,32,256]{3,2,1,0:T(8,128)(2,1)S(1)} %get-tuple-element.11), channel_id=1, source_target_pairs={{0,4},{4,8},{8,12},{12,16},{16,20},{20,24},{24,28},{28,32},{32,36}... | collective-permute-start | bytes 1572872 | tf_op jit(solution)/shard_map/ppermute | solution.py:619
  21.1 57.7 %collective-permute-start.1 = (bf16[1,32,32,256]{3,2,1,0:T(8,128)(2,1)S(1)}, bf16[1,32,32,256]{3,2,1,0:T(8,128)(2,1)S(1)}, u32[]{:S(2)}, u32[]{:S(2)}) collective-permute-start(bf16[1,32,32,256]{3,2,1,0:T(8,128)(2,1)S(1)} %get-tuple-element.10), channel_id=1, source_target_pairs={{4,0},{8,4},{12,8},{16,12},{20,16},{24,20},{28,24},{32,28},{36,32}... | collective-permute-start | bytes 1572872 | tf_op jit(solution)/shard_map/ppermute | solution.py:620
  78.8 0.8 copy-start.6
  79.6 0.8 copy-start.7
  109.7 15.7 %copy-start = (bf16[128,1024]{1,0:T(8,128)(2,1)S(1)}, bf16[128,1024]{1,0:T(8,128)(2,1)}, u32[]{:S(2)}) copy-start(bf16[128,1024]{1,0:T(8,128)(2,1)} %keys_ref.1) | copy-start | bytes 786436
  109.7 15.7 %copy-start.1 = (f32[128,256]{1,0:T(8,128)S(1)}, f32[128,256]{1,0:T(8,128)}, u32[]{:S(2)}) copy-start(f32[128,256]{1,0:T(8,128)} %latents_ref.1) | copy-start | bytes 393220
  109.7 15.7 %copy-start.2 = (f32[1024]{0:T(1024)S(1)}, f32[1024]{0:T(1024)}, u32[]{:S(2)}) copy-start(f32[1024]{0:T(1024)} %param.15) | copy-start | bytes 12292
  125.4 93.9 %copy-start.3 = (bf16[8192,256]{1,0:T(8,128)(2,1)S(1)}, bf16[8192,256]{1,0:T(8,128)(2,1)}, u32[]{:S(2)}) copy-start(bf16[8192,256]{1,0:T(8,128)(2,1)} %scatter.1.mixed_ref) | copy-start | bytes 12582916

commit v4 on v3

--- a/solution.py
+++ b/solution.py
@@ -29,7 +29,6 @@
     nothing = coded(jnp.full((1, rows), empty, jnp.int32))
 
     def clear(j, carry):
-        out_ref[j, pl.ds(0, rows), :] = jnp.zeros((rows, width), BF16)
         out_ref[j, pl.ds(rows, EXTRA), :] = nothing
         return carry
 
@@ -137,14 +136,33 @@
 
 
 def scatter_kernel(
-    spots_ref, clash_ref, base_ref, recv_ref, out_ref, acc, wide, feat, feat_sems, base_sem
+    base_ref,
+    recv_ref,
+    out_ref,
+    acc,
+    wide,
+    feat,
+    codes,
+    spots,
+    clash,
+    out,
+    spots_ref,
+    clash_ref,
+    feat_sems,
+    base_sem,
+    code_sems,
+    out_sems,
 ):
-    slots, block_rows = spots_ref.shape
+    slots, block_rows, _ = feat.shape
     total = acc.shape[0] // 2
     pieces = feat_sems.shape[0]
     each = slots // pieces
     step = 128
 
+    code_copy = pltpu.make_async_copy(
+        recv_ref.at[pl.ds(0, slots), pl.ds(block_rows, EXTRA)], codes, code_sems.at[0]
+    )
+    code_copy.start()
     base_copy = pltpu.make_async_copy(base_ref, acc, base_sem)
 
     def fetch(i):
@@ -157,6 +175,30 @@
     base_copy.start()
     for i in range(pieces):
         fetch(i).start()
+
+    code_copy.wait()
+    code = jnp.max(codes[...].astype(F32), axis=1)
+    number = (code[:, :block_rows] * 128.0 + code[:, block_rows:]).astype(jnp.int32)
+    spots[...] = (number // 8) * 16 + number % 8
+    lane = lax.broadcasted_iota(jnp.int32, number.shape, 1)
+    again = jnp.zeros_like(number)
+    for k in range(1, GROUP):
+        same = (number == pltpu.roll(number, k, 1)) & (lane % GROUP >= k)
+        again = jnp.where(same, 1, again)
+    k = 1
+    while k < GROUP:
+        again = jnp.maximum(again, jnp.where(lane % GROUP >= k, pltpu.roll(again, k, 1), 0))
+        k *= 2
+    most = jnp.max(again.astype(F32), axis=1, keepdims=True).astype(jnp.int32)
+    clash[...] = jnp.where(lane == 0, most, again)
+    scalars = (
+        pltpu.make_async_copy(spots, spots_ref, code_sems.at[1]),
+        pltpu.make_async_copy(clash, clash_ref, code_sems.at[2]),
+    )
+    for copy in scalars:
+        copy.start()
+    for copy in scalars:
+        copy.wait()
     base_copy.wait()
 
     def at(spot):
@@ -185,20 +227,20 @@
                 for r, new in zip(where, news):
                     acc[at(r), :] = new
 
-            @pl.when(clash_ref[j, groups] == 0)
+            @pl.when(clash_ref[j, 0] == 0)
             def _():
                 for g in range(groups):
                     together(g)
 
-            @pl.when(clash_ref[j, groups] != 0)
+            @pl.when(clash_ref[j, 0] != 0)
             def _():
                 for g in range(groups):
 
-                    @pl.when(clash_ref[j, g] == 0)
+                    @pl.when(clash_ref[j, (g + 1) * GROUP - 1] == 0)
                     def _():
                         together(g)
 
-                    @pl.when(clash_ref[j, g] != 0)
+                    @pl.when(clash_ref[j, (g + 1) * GROUP - 1] != 0)
                     def _():
                         for c in range(g * GROUP, (g + 1) * GROUP):
                             r = spots_ref[j, c]
@@ -213,35 +255,52 @@
         value = value.reshape(step // 8, 2, 8, 128)
         part = pl.ds(pl.multiple_of(i * step, step), step)
         for h in range(2):
-            out_ref[part, 128 * h : 128 * h + 128] = value[:, h].reshape(step, 128).astype(BF16)
-        return carry
-
-    lax.fori_loop(0, total // step, finish, 0)
-
-
-def scatter(spots, clash, base, recv):
+            out[part, 128 * h : 128 * h + 128] = value[:, h].reshape(step, 128).astype(BF16)
+        return carry
+
+    parts = out_sems.shape[0]
+    share = total // parts
+
+    def out_copy(p):
+        rows = pl.ds(p * share, share)
+        return pltpu.make_async_copy(out.at[rows], out_ref.at[rows], out_sems.at[p])
+
+    for p in range(parts):
+        lax.fori_loop(p * share // step, (p + 1) * share // step, finish, 0)
+        out_copy(p).start()
+    for p in range(parts):
+        out_copy(p).wait()
+
+
+def scatter(base, recv):
     total, width = base.shape[0] // 2, 2 * base.shape[1]
-    slots, block_rows = spots.shape
+    slots, block_rows = recv.shape[0], recv.shape[1] - EXTRA
+    anywhere = pl.BlockSpec(memory_space=pl.ANY)
+    dma = pltpu.SemaphoreType.DMA
     return pl.pallas_call(
         scatter_kernel,
         out_shape=jax.ShapeDtypeStruct((total, width), BF16),
-        in_specs=[
-            pl.BlockSpec(memory_space=pltpu.SMEM),
-            pl.BlockSpec(memory_space=pltpu.SMEM),
-            pl.BlockSpec(memory_space=pl.ANY),
-            pl.BlockSpec(memory_space=pl.ANY),
-        ],
-        out_specs=whole(),
+        in_specs=[anywhere, anywhere],
+        out_specs=anywhere,
         scratch_shapes=[
             pltpu.VMEM((2 * total, 128), F32),
             pltpu.VMEM((2 * block_rows, 128), F32),
             pltpu.VMEM((slots, block_rows, width), BF16),
-            pltpu.SemaphoreType.DMA((8,)),
-            pltpu.SemaphoreType.DMA,
+            pltpu.VMEM((slots, EXTRA, width), BF16),
+            pltpu.VMEM((slots, block_rows), jnp.int32),
+            pltpu.VMEM((slots, block_rows), jnp.int32),
+            pltpu.VMEM((total, width), BF16),
+            pltpu.SMEM((slots, block_rows), jnp.int32),
+            pltpu.SMEM((slots, block_rows), jnp.int32),
+            dma((8,)),
+            dma,
+            dma((3,)),
+            dma((4,)),
         ],
+        compiler_params=pltpu.CompilerParams(vmem_limit_bytes=60 << 20),
         cost_estimate=pl.CostEstimate(flops=2 << 20, bytes_accessed=16 << 20, transcendentals=0),
         name="scatter",
-    )(spots, clash, base, recv)
+    )(base, recv)
 
 
 CHUNKS = 8
@@ -312,14 +371,19 @@
         for where in (slab, far_slab):
             pl.semaphore_signal(barrier, inc=1, device_id=(where, peers[d]), device_id_type=MESH)
 
+    pl.semaphore_signal(barrier, inc=1, device_id=(far_slab, chan), device_id_type=MESH)
+
     def greet(k, carry):
         pl.semaphore_signal(
-            barrier, inc=1, device_id=((slab + k) % slabs, chan), device_id_type=MESH
-        )
-        return carry
-
-    lax.fori_loop(1, slabs, greet, 0)
-    pl.semaphore_wait(barrier, 6 + slabs - 1)
+            barrier,
+            inc=1,
+            device_id=(z_hi * half + (spot + k) % half, chan),
+            device_id_type=MESH,
+        )
+        return carry
+
+    lax.fori_loop(1, half, greet, 0)
+    pl.semaphore_wait(barrier, 7 + half - 1)
 
     def x_copy(d, i):
         rows = pl.ds(i * size, size)
@@ -420,64 +484,60 @@
     pool_chunk(CHUNKS - 1)
 
     column = [(far, d) for far in range(2) for d in range(4)][1:]
-    held = pooled.shape[1] // 2
+    held = pooled.shape[1]
+    place = z_hi * 4 + chan
 
     def p_copy(n):
         far, d = column[n]
         return pltpu.make_async_remote_copy(
-            src_ref=part_out.at[(z_hi + far) % 2, peers[d]],
-            dst_ref=part_in.at[n],
+            src_ref=part_out.at[peers[d]],
+            dst_ref=part_in.at[place],
             send_sem=p_send.at[n],
             recv_sem=p_recv.at[n],
             device_id=((slab + far * half) % slabs, peers[d]),
             device_id_type=MESH,
         )
 
-    weights = totals[...]
+    weights = totals[...].astype(BF16)
     for p in range(4):
-        for h in range(2):
-            part_out[h, p, pl.ds(0, held)] = pooled[p, pl.ds(h * held, held)].astype(BF16)
-            part_out[h, p, pl.ds(held, 16), pl.ds(0, 128)] = weights.astype(BF16)
-            part_out[h, p, pl.ds(held, 16), pl.ds(128, width - 128)] = jnp.zeros(
-                (16, width - 128), BF16
-            )
-    for n in (1, 2, 3, 4, 5, 6, 0):
+        part_out[p, pl.ds(0, held)] = pooled[p].astype(BF16)
+        part_out[p, pl.ds(held, 16), pl.ds(0, 128)] = weights
+        part_out[p, pl.ds(held, 16), pl.ds(128, width - 128)] = jnp.zeros((16, width - 128), BF16)
+    for n in (4, 1, 2, 5, 6, 3, 0):
         p_copy(n).start()
     for d in (2, 1):
         a_copy(d).start()
     keep = pltpu.make_async_copy(own, assign_ref.at[pl.ds(chan * quarter, quarter)], local_sem.at[0])
     keep.start()
+    part_in[place] = part_out[chan]
     for n in range(7):
         p_copy(n).wait_recv()
-    mine = pooled[chan, pl.ds(pl.multiple_of(z_hi * held, held), held)]
-    for n in range(7):
+    mine = part_in[0, pl.ds(0, held)].astype(F32)
+    total = part_in[0, pl.ds(held, 16), pl.ds(0, 128)].astype(F32)
+    for n in range(1, 8):
         mine = mine + part_in[n, pl.ds(0, held)].astype(F32)
-        weights = weights + part_in[n, pl.ds(held, 16), pl.ds(0, 128)].astype(F32)
+        total = total + part_in[n, pl.ds(held, 16), pl.ds(0, 128)].astype(F32)
 
     for t in range(half):
-        tile_out[t, 0] = mine[8 * (t // 2) : 8 * (t // 2) + 8, 128 * (t % 2) : 128 * (t % 2) + 128]
-        tile_out[t, 1] = weights[:8]
+        for h in range(2):
+            tile_out[t, h] = mine[8 * t : 8 * t + 8, 128 * h : 128 * h + 128]
+        tile_out[t, 2] = total[:8]
+
+    def plane_copy(k, source, target, send, recv):
+        return pltpu.make_async_remote_copy(
+            src_ref=source,
+            dst_ref=target.at[spot],
+            send_sem=send.at[k - 1],
+            recv_sem=recv.at[k - 1],
+            device_id=(z_hi * half + (spot + k) % half, chan),
+            device_id_type=MESH,
+        )
 
     def t_copy(k):
-        to = (spot + k) % half
-        return pltpu.make_async_remote_copy(
-            src_ref=tile_out.at[to],
-            dst_ref=tile_in.at[spot],
-            send_sem=t_send.at[k - 1],
-            recv_sem=t_recv.at[k - 1],
-            device_id=(z_hi * half + to, chan),
-            device_id_type=MESH,
-        )
+        return plane_copy(k, tile_out.at[(spot + k) % half], tile_in, t_send, t_recv)
 
     def n_copy(k):
-        return pltpu.make_async_remote_copy(
-            src_ref=new_out,
-            dst_ref=new_in.at[slab],
-            send_sem=n_send.at[k - 1],
-            recv_sem=n_recv.at[k - 1],
-            device_id=((slab + k) % slabs, chan),
-            device_id_type=MESH,
-        )
+        return plane_copy(k, new_out, new_in, n_send, n_recv)
 
     def over(number, action):
         def body(k, carry):
@@ -490,17 +550,17 @@
     tile_in[spot] = tile_out[spot]
     over(half, lambda k: t_copy(k).wait_recv())
     sums = jnp.sum(tile_in[...], axis=0)
-    first = z_hi * held + 8 * (spot // 2)
+    first = 8 * spot
     row = lax.broadcasted_iota(jnp.int32, (8, 128), 0)
     lane = lax.broadcasted_iota(jnp.int32, (8, 128), 1)
-    weight = jnp.sum(jnp.where(lane == row + first, sums[1], 0.0), axis=1, keepdims=True)
-    before = latents_ref[
-        pl.ds(pl.multiple_of(first, 8), 8), pl.ds(pl.multiple_of(128 * (spot % 2), 128), 128)
-    ]
-    fresh = before + sums[0] / (weight + 1.0)
-    new_out[...] = fresh
-    over(slabs, lambda k: n_copy(k).start())
-    new_in[slab] = fresh
+    weight = jnp.sum(jnp.where(lane == row + first, sums[2], 0.0), axis=1, keepdims=True)
+    for h in range(2):
+        before = latents_ref[
+            pl.ds(pl.multiple_of(first, 8), 8), pl.ds(128 * h, 128)
+        ]
+        new_out[h] = before + sums[h] / (weight + 1.0)
+    over(half, lambda k: n_copy(k).start())
+    new_in[spot] = new_out[...]
 
     def forward():
         rows = pl.ds(peers[2] * quarter, quarter)
@@ -516,10 +576,10 @@
     a_copy(2).wait_recv()
     forward().start()
 
-    over(slabs, lambda k: n_copy(k).wait_recv())
-    for t in range(slabs):
-        top, left = held * (t // half) + 8 * ((t % half) // 2), 128 * (t % 2)
-        latent_ref[top : top + 8, left : left + 128] = new_in[t]
+    over(half, lambda k: n_copy(k).wait_recv())
+    for t in range(half):
+        for h in range(2):
+            latent_ref[8 * t : 8 * t + 8, 128 * h : 128 * h + 128] = new_in[t, h]
 
     def drained(i, carry):
         for d in (1, 2, 3):
@@ -532,7 +592,7 @@
     for n in range(7):
         p_copy(n).wait_send()
     over(half, lambda k: t_copy(k).wait_send())
-    over(slabs, lambda k: n_copy(k).wait_send())
+    over(half, lambda k: n_copy(k).wait_send())
     a_copy(1).wait_recv()
     for d in (1, 2):
         a_copy(d).wait_send()
@@ -567,12 +627,12 @@
             pltpu.VMEM((quarter, held), BF16),
             pltpu.VMEM((4, held, width), F32),
             pltpu.VMEM((16, 128), F32),
-            pltpu.VMEM((2, 4, held // 2 + 16, width), BF16),
-            pltpu.VMEM((7, held // 2 + 16, width), BF16),
+            pltpu.VMEM((4, held + 16, width), BF16),
+            pltpu.VMEM((8, held + 16, width), BF16),
+            pltpu.VMEM((slabs // 2, 3, 8, 128), F32),
+            pltpu.VMEM((slabs // 2, 3, 8, 128), F32),
+            pltpu.VMEM((2, 8, 128), F32),
             pltpu.VMEM((slabs // 2, 2, 8, 128), F32),
-            pltpu.VMEM((slabs // 2, 2, 8, 128), F32),
-            pltpu.VMEM((8, 128), F32),
-            pltpu.VMEM((slabs, 8, 128), F32),
             dma((2,)),
             dma((3, CHUNKS)),
             dma((3, CHUNKS)),
@@ -584,8 +644,8 @@
             dma((7,)),
             dma((slabs // 2 - 1,)),
             dma((slabs // 2 - 1,)),
-            dma((slabs - 1,)),
-            dma((slabs - 1,)),
+            dma((slabs // 2 - 1,)),
+            dma((slabs // 2 - 1,)),
         ],
         compiler_params=pltpu.CompilerParams(
             collective_id=0, has_side_effects=True, vmem_limit_bytes=48 << 20
@@ -632,16 +692,7 @@
     base = conv(tokens, before, after, conv_w)
     weights = jnp.concatenate([w_val, w_gate], axis=1)
 
-    got = received[:, block_rows, :].astype(jnp.int32)
-    rows = got[:, :block_rows] * 128 + got[:, block_rows:]
-    grouped = rows.reshape(slots, block_rows // GROUP, GROUP)
-    same = grouped[..., :, None] == grouped[..., None, :]
-    above = jnp.arange(GROUP)[:, None] < jnp.arange(GROUP)[None, :]
-    clash = jnp.any(same & above, axis=(2, 3))
-    clash = jnp.concatenate([clash, jnp.any(clash, axis=1, keepdims=True)], axis=1).astype(jnp.int32)
-
-    spots = (rows // 8) * 16 + rows % 8
-    mixed = scatter(spots, clash, base, received)
+    mixed = scatter(base, received)
     assign, latent_new = mix(mixed, weights, latent_keys, norm_gain[None, :], latents)
     readback = jnp.dot(assign, latent_new.astype(BF16), preferred_element_type=F32)
     block_out = (mixed.astype(F32) + readback).astype(BF16)

time: 225 us -> 219 us (0.973)
  Pallas kernels: 141 us -> 137 us
    pallas_call x1, Pallas kernels: 15.7 us -> 13.4 us  [scatter(): pl.pallas_call(scatter_kernel, out_shape=jax.ShapeDtypeStruct((total, wid...]
where the time goes in v4:
time: 219 us; the launch traced here: 216 us
  Pallas kernels  137 us (63%)
  waiting for transfers between devices  56.3 us (26%)
  starting transfers between devices  15.9 us (7%)
  local copies, waits for them, and re-layouts  3.53 us (2%)
  matrix products  3.25 us (1%)
    pallas_call x1, Pallas kernels, mix(): pl.pallas_call(mix_kernel, out_shape=(jax.ShapeDtypeStruct((rows, held),...  92.3 us
    ppermute x1, waiting for transfers between devices, per_device(): before = lax.ppermute(tokens[-1:], 'slab', up)  56.3 us
    pallas_call x1, Pallas kernels, conv(): pl.pallas_call(conv_kernel, grid=(depth,), out_shape=jax.ShapeDtypeStruct...  26.4 us
    pallas_call x1, Pallas kernels, scatter(): pl.pallas_call(scatter_kernel, out_shape=jax.ShapeDtypeStruct((total, wid...  13.4 us
    all_to_all x1, starting transfers between devices, per_device(): lax.all_to_all(sent.reshape(slabs, capacity * (block_rows + EXTRA), width...  11 us
    pallas_call x1, Pallas kernels, pack(): pl.pallas_call(functools.partial(pack_kernel, capacity, empty), out_shape...  4.45 us
  transfers between devices with their start and end apart: 3, of which 1 were waited for; matrix products, arithmetic and copies ran while one was open for 1% of the time, Pallas kernels for 12%

profile of v4, /device:TPU:0, one launch (start us, length us, event | category | flops | bytes accessed | tf_op | source)
XLA Modules:
  0.0 216.4 jit_solution(10803108065857978283)
XLA Ops:
  0.6 4.4 %pack.1 = bf16[64,136,256]{2,1,0:T(8,128)(2,1)} custom-call(s32[32]{0:T(128)} %bitcast.9, bf16[32,128,256]{2,1,0:T(8,128)(2,1)} %feat_ref.1, s32[32,128]{1,0:T(8,128)} %rows_ref.1), custom_call_target="tpu_custom_call" | custom-call | bytes 6291456 | tf_op jit(solution)/shard_map/pack/pallas_call | solution.py:53
  5.1 11.0 %all-to-all-start = ((bf16[32,272,256]{2,1,0:T(8,128)(2,1)}), bf16[32,272,256]{2,1,0:T(8,128)(2,1)}, u32[]{:S(2)}, u32[]{:S(2)}) async-start(bf16[32,272,256]{2,1,0:T(8,128)(2,1)} %bitcast.7), calls=%async_computation | async-start | bytes 8912896 | tf_op jit(solution)/shard_map/all_to_all | solution.py:683
  16.1 1.3 fusion.4
  17.4 3.7 %collective-permute-start = (bf16[1,32,32,256]{3,2,1,0:T(8,128)(2,1)S(1)}, bf16[1,32,32,256]{3,2,1,0:T(8,128)(2,1)S(1)}, u32[]{:S(2)}, u32[]{:S(2)}) collective-permute-start(bf16[1,32,32,256]{3,2,1,0:T(8,128)(2,1)S(1)} %get-tuple-element.7), channel_id=1, source_target_pairs={{0,4},{4,8},{8,12},{12,16},{16,20},{20,24},{24,28},{28,32},{32,36}... | collective-permute-start | bytes 1572872 | tf_op jit(solution)/shard_map/ppermute | solution.py:679
  21.0 1.3 collective-permute-start.1
  22.3 0.0 copy-done.4
  22.3 0.0 copy-done.5
  22.3 0.1 pad_maximum_fusion.w_ref
  22.4 56.3 %collective-permute-done.before_ref = bf16[1,32,32,256]{3,2,1,0:T(8,128)(2,1)S(1)} collective-permute-done((bf16[1,32,32,256]{3,2,1,0:T(8,128)(2,1)S(1)}, bf16[1,32,32,256]{3,2,1,0:T(8,128)(2,1)S(1)}, u32[]{:S(2)}, u32[]{:S(2)}) %collective-permute-start) | collective-permute-done | bytes 524320 | tf_op jit(solution)/shard_map/ppermute | solution.py:679
  78.7 0.0 collective-permute-done.1.after_ref
  78.7 0.8 copy-done.6
  79.5 0.8 copy-done.7
  80.3 26.4 %conv.1.base_ref = f32[16384,128]{1,0:T(8,128)} custom-call(bf16[8,32,32,256]{3,2,1,0:T(8,128)(2,1)} %tokens_ref.1, bf16[1,32,32,256]{3,2,1,0:T(8,128)(2,1)} %copy-done.6, bf16[1,32,32,256]{3,2,1,0:T(8,128)(2,1)} %copy-done.7, f32[27,256]{1,0:T(8,128)} %w_ref.1), custom_call_target="tpu_custom_call" | custom-call | flops 113246208 | bytes 31457280 | tf_op jit(solution)/shard_map/conv/pallas_call | solution.py:121
  106.7 0.0 all-to-all-done
  106.7 0.0 copy-start.2
  106.8 13.4 %scatter.1.mixed_ref = bf16[8192,256]{1,0:T(8,128)(2,1)} custom-call(f32[16384,128]{1,0:T(8,128)} %conv.1.base_ref, bf16[64,136,256]{2,1,0:T(8,128)(2,1)} %bitcast.2.recv_ref), custom_call_target="tpu_custom_call" | custom-call | flops 2097152 | bytes 16777216 | tf_op jit(solution)/shard_map/scatter/pallas_call | solution.py:280
  120.2 0.0 copy-done
  120.2 0.0 copy-done.1
  120.2 0.0 copy-done.2
  120.2 0.0 copy-start.3
  120.2 92.3 %mix.1 = (bf16[8192,128]{1,0:T(8,128)(2,1)S(1)}, f32[128,256]{1,0:T(8,128)S(1)}) custom-call(bf16[8192,256]{1,0:T(8,128)(2,1)} %scatter.1.mixed_ref, bf16[1024,512]{1,0:T(8,128)(2,1)S(1)} %pad_maximum_fusion.w_ref, bf16[128,1024]{1,0:T(8,128)(2,1)S(1)} %copy-done, f32[1,1024]{1,0:T(1,128)S(1)} %bitcast.6, f32[128,256]{1,0:T(8,128)S(1)} %copy-done.1), custom_call_target="tpu_custom_call" | custom-call | flops 10737418240 | bytes 16777216 | tf_op jit(solution)/shard_map/mix/pallas_call | solution.py:609
  212.5 0.0 copy-done.3
  212.5 3.2 %add_convert_fusion = bf16[8192,256]{1,0:T(8,128)(2,1)} fusion(bf16[8192,256]{1,0:T(8,128)(2,1)S(1)} %copy-done.3, bf16[8192,128]{1,0:T(8,128)(2,1)S(1)} %get-tuple-element.4, f32[128,256]{1,0:T(8,128)S(1)} %get-tuple-element.11), kind=kOutput, calls=%fused_computation | convolution fusion | flops 543195136 | bytes 10616832 | tf_op jit(solution)/shard_map/dot_general | solution.py:697
  215.8 0.7 copy.13
  (6 shorter events, 0.0 us)
Async XLA Ops:
  5.1 17.2 %copy-start.4 = (bf16[1024,256]{1,0:T(8,128)(2,1)S(1)}, bf16[1024,256]{1,0:T(8,128)(2,1)}, u32[]{:S(2)}) copy-start(bf16[1024,256]{1,0:T(8,128)(2,1)} %param.17) | copy-start | bytes 1572868
  5.1 17.3 %copy-start.5 = (bf16[1024,256]{1,0:T(8,128)(2,1)S(1)}, bf16[1024,256]{1,0:T(8,128)(2,1)}, u32[]{:S(2)}) copy-start(bf16[1024,256]{1,0:T(8,128)(2,1)} %param.16) | copy-start | bytes 1572868
  5.1 101.6 %all-to-all-start = ((bf16[32,272,256]{2,1,0:T(8,128)(2,1)}), bf16[32,272,256]{2,1,0:T(8,128)(2,1)}, u32[]{:S(2)}, u32[]{:S(2)}) async-start(bf16[32,272,256]{2,1,0:T(8,128)(2,1)} %bitcast.7), calls=%async_computation | async-start | bytes 8912896 | tf_op jit(solution)/shard_map/all_to_all | solution.py:683
  17.4 61.3 %collective-permute-start = (bf16[1,32,32,256]{3,2,1,0:T(8,128)(2,1)S(1)}, bf16[1,32,32,256]{3,2,1,0:T(8,128)(2,1)S(1)}, u32[]{:S(2)}, u32[]{:S(2)}) collective-permute-start(bf16[1,32,32,256]{3,2,1,0:T(8,128)(2,1)S(1)} %get-tuple-element.7), channel_id=1, source_target_pairs={{0,4},{4,8},{8,12},{12,16},{16,20},{20,24},{24,28},{28,32},{32,36}... | collective-permute-start | bytes 1572872 | tf_op jit(solution)/shard_map/ppermute | solution.py:679
  21.0 57.7 %collective-permute-start.1 = (bf16[1,32,32,256]{3,2,1,0:T(8,128)(2,1)S(1)}, bf16[1,32,32,256]{3,2,1,0:T(8,128)(2,1)S(1)}, u32[]{:S(2)}, u32[]{:S(2)}) collective-permute-start(bf16[1,32,32,256]{3,2,1,0:T(8,128)(2,1)S(1)} %get-tuple-element.6), channel_id=1, source_target_pairs={{4,0},{8,4},{12,8},{16,12},{20,16},{24,20},{28,24},{32,28},{36,32}... | collective-permute-start | bytes 1572872 | tf_op jit(solution)/shard_map/ppermute | solution.py:680
  78.7 0.8 copy-start.6
  79.5 0.8 copy-start.7
  106.7 13.5 %copy-start = (bf16[128,1024]{1,0:T(8,128)(2,1)S(1)}, bf16[128,1024]{1,0:T(8,128)(2,1)}, u32[]{:S(2)}) copy-start(bf16[128,1024]{1,0:T(8,128)(2,1)} %keys_ref.1) | copy-start | bytes 786436
  106.7 13.5 %copy-start.1 = (f32[128,256]{1,0:T(8,128)S(1)}, f32[128,256]{1,0:T(8,128)}, u32[]{:S(2)}) copy-start(f32[128,256]{1,0:T(8,128)} %latents_ref.1) | copy-start | bytes 393220
  106.7 13.5 %copy-start.2 = (f32[1024]{0:T(1024)S(1)}, f32[1024]{0:T(1024)}, u32[]{:S(2)}) copy-start(f32[1024]{0:T(1024)} %param.15) | copy-start | bytes 12292
  120.2 92.3 %copy-start.3 = (bf16[8192,256]{1,0:T(8,128)(2,1)S(1)}, bf16[8192,256]{1,0:T(8,128)(2,1)}, u32[]{:S(2)}) copy-start(bf16[8192,256]{1,0:T(8,128)(2,1)} %scatter.1.mixed_ref) | copy-start | bytes 12582916

commit v5 on v4

--- a/solution.py
+++ b/solution.py
@@ -18,9 +18,20 @@
     return pl.BlockSpec(memory_space=pltpu.VMEM)
 
 
-def pack_kernel(capacity, empty, dest_ref, feat_ref, rows_ref, out_ref, taken):
-    slots, width = out_ref.shape[0], out_ref.shape[2]
+def pack_kernel(
+    capacity, empty, dest_ref, feat_ref, rows_ref, out_ref, taken, slot_of, feat, codes, in_sems, out_sems, code_sem
+):
+    slots, _, width = out_ref.shape
     blocks, rows, _ = feat_ref.shape
+    pieces = in_sems.shape[0]
+    each = blocks // pieces
+
+    def fetch(i):
+        part = pl.ds(i * each, each)
+        return pltpu.make_async_copy(feat_ref.at[part], feat.at[part], in_sems.at[i])
+
+    for i in range(pieces):
+        fetch(i).start()
 
     def coded(number):
         both = jnp.concatenate([number // 128, number % 128], axis=1)
@@ -29,33 +40,67 @@
     nothing = coded(jnp.full((1, rows), empty, jnp.int32))
 
     def clear(j, carry):
-        out_ref[j, pl.ds(rows, EXTRA), :] = nothing
+        codes[j] = nothing
         return carry
 
     lax.fori_loop(0, slots, clear, 0)
     for t in range(slots // capacity):
         taken[t] = 0
 
-    def one(b, carry):
+    def place(b, carry):
         to = dest_ref[b]
         slot = to * capacity + taken[to]
         taken[to] = taken[to] + 1
-        out_ref[slot, pl.ds(0, rows), :] = feat_ref[b]
-        out_ref[slot, pl.ds(rows, EXTRA), :] = coded(rows_ref[pl.ds(b, 1), :])
-        return carry
-
-    lax.fori_loop(0, blocks, one, 0)
+        slot_of[b] = slot
+        codes[slot] = coded(rows_ref[pl.ds(b, 1), :])
+        return carry
+
+    lax.fori_loop(0, blocks, place, 0)
+    code_copy = pltpu.make_async_copy(
+        codes, out_ref.at[pl.ds(0, slots), pl.ds(rows, EXTRA)], code_sem
+    )
+    code_copy.start()
+
+    def put(b):
+        return pltpu.make_async_copy(
+            feat.at[b], out_ref.at[slot_of[b], pl.ds(0, rows)], out_sems.at[b]
+        )
+
+    def send(b, carry):
+        put(b).start()
+        return carry
+
+    def finish(b, carry):
+        put(b).wait()
+        return carry
+
+    for i in range(pieces):
+        fetch(i).wait()
+        lax.fori_loop(i * each, (i + 1) * each, send, 0)
+    lax.fori_loop(0, blocks, finish, 0)
+    code_copy.wait()
 
 
 def pack(dest, feat, row_ids, slabs, capacity, empty):
-    _, rows, width = feat.shape
+    blocks, rows, width = feat.shape
     slots = slabs * capacity
+    anywhere = pl.BlockSpec(memory_space=pl.ANY)
+    dma = pltpu.SemaphoreType.DMA
     return pl.pallas_call(
         functools.partial(pack_kernel, capacity, empty),
         out_shape=jax.ShapeDtypeStruct((slots, rows + EXTRA, width), BF16),
-        in_specs=[pl.BlockSpec(memory_space=pltpu.SMEM), whole(), whole()],
-        out_specs=whole(),
-        scratch_shapes=[pltpu.SMEM((slabs,), jnp.int32)],
+        in_specs=[pl.BlockSpec(memory_space=pltpu.SMEM), anywhere, whole()],
+        out_specs=anywhere,
+        scratch_shapes=[
+            pltpu.SMEM((slabs,), jnp.int32),
+            pltpu.SMEM((blocks,), jnp.int32),
+            pltpu.VMEM(feat.shape, BF16),
+            pltpu.VMEM((slots, EXTRA, width), BF16),
+            dma((4,)),
+            dma((blocks,)),
+            dma,
+        ],
+        compiler_params=pltpu.CompilerParams(vmem_limit_bytes=60 << 20),
         cost_estimate=pl.CostEstimate(flops=0, bytes_accessed=6 << 20, transcendentals=0),
         name="pack",
     )(dest, feat, row_ids)
@@ -411,12 +456,14 @@
             device_id_type=MESH,
         )
 
-    def a_copy(d):
+    part_rows = quarter // 2
+
+    def a_copy(d, i):
         return pltpu.make_async_remote_copy(
-            src_ref=own,
-            dst_ref=assign_ref.at[pl.ds(chan * quarter, quarter)],
-            send_sem=a_send.at[d - 1],
-            recv_sem=a_recv.at[d - 1],
+            src_ref=own.at[pl.ds(i * part_rows, part_rows)],
+            dst_ref=assign_ref.at[pl.ds(chan * quarter + i * part_rows, part_rows)],
+            send_sem=a_send.at[d - 1, i],
+            recv_sem=a_recv.at[d - 1, i],
             device_id=(slab, peers[d]),
             device_id_type=MESH,
         )
@@ -505,8 +552,9 @@
         part_out[p, pl.ds(held, 16), pl.ds(128, width - 128)] = jnp.zeros((16, width - 128), BF16)
     for n in (4, 1, 2, 5, 6, 3, 0):
         p_copy(n).start()
-    for d in (2, 1):
-        a_copy(d).start()
+    for i in range(2):
+        for d in (2, 1):
+            a_copy(d, i).start()
     keep = pltpu.make_async_copy(own, assign_ref.at[pl.ds(chan * quarter, quarter)], local_sem.at[0])
     keep.start()
     part_in[place] = part_out[chan]
@@ -562,19 +610,20 @@
     over(half, lambda k: n_copy(k).start())
     new_in[spot] = new_out[...]
 
-    def forward():
-        rows = pl.ds(peers[2] * quarter, quarter)
+    def forward(i):
+        rows = pl.ds(peers[2] * quarter + i * part_rows, part_rows)
         return pltpu.make_async_remote_copy(
             src_ref=assign_ref.at[rows],
             dst_ref=assign_ref.at[rows],
-            send_sem=a_send.at[2],
-            recv_sem=a_recv.at[2],
+            send_sem=a_send.at[2, i],
+            recv_sem=a_recv.at[2, i],
             device_id=(slab, peers[1]),
             device_id_type=MESH,
         )
 
-    a_copy(2).wait_recv()
-    forward().start()
+    for i in range(2):
+        a_copy(2, i).wait_recv()
+        forward(i).start()
 
     over(half, lambda k: n_copy(k).wait_recv())
     for t in range(half):
@@ -593,10 +642,11 @@
         p_copy(n).wait_send()
     over(half, lambda k: t_copy(k).wait_send())
     over(half, lambda k: n_copy(k).wait_send())
-    a_copy(1).wait_recv()
-    for d in (1, 2):
-        a_copy(d).wait_send()
-    forward().wait()
+    for i in range(2):
+        a_copy(1, i).wait_recv()
+        for d in (1, 2):
+            a_copy(d, i).wait_send()
+        forward(i).wait()
     keep.wait()
 
 
@@ -638,8 +688,8 @@
             dma((3, CHUNKS)),
             dma((3,)),
             dma((3,)),
-            dma((3,)),
-            dma((3,)),
+            dma((3, 2)),
+            dma((3, 2)),
             dma((7,)),
             dma((7,)),
             dma((slabs // 2 - 1,)),

time: 219 us -> 218 us (level)
  no operation moved by 1% of the time
where the time goes in v5:
time: 218 us; the launch traced here: 216 us
  Pallas kernels  136 us (62%)
  waiting for transfers between devices  56.3 us (26%)
  starting transfers between devices  16 us (7%)
  local copies, waits for them, and re-layouts  3.54 us (2%)
  matrix products  3.25 us (1%)
    pallas_call x1, Pallas kernels, mix(): pl.pallas_call(mix_kernel, out_shape=(jax.ShapeDtypeStruct((rows, held),...  92.4 us
    ppermute x1, waiting for transfers between devices, per_device(): before = lax.ppermute(tokens[-1:], 'slab', up)  56.3 us
    pallas_call x1, Pallas kernels, conv(): pl.pallas_call(conv_kernel, grid=(depth,), out_shape=jax.ShapeDtypeStruct...  26.4 us
    pallas_call x1, Pallas kernels, scatter(): pl.pallas_call(scatter_kernel, out_shape=jax.ShapeDtypeStruct((total, wid...  13.4 us
    all_to_all x1, starting transfers between devices, per_device(): lax.all_to_all(sent.reshape(slabs, capacity * (block_rows + EXTRA), width...  11 us
  transfers between devices with their start and end apart: 3, of which 1 were waited for; matrix products, arithmetic and copies ran while one was open for 1% of the time, Pallas kernels for 12%

profile of v5, /device:TPU:0, one launch (start us, length us, event | category | flops | bytes accessed | tf_op | source)
XLA Modules:
  0.0 215.6 jit_solution(18037838417013855117)
XLA Ops:
  0.6 3.5 %pack.1 = bf16[64,136,256]{2,1,0:T(8,128)(2,1)} custom-call(s32[32]{0:T(128)} %bitcast.9, bf16[32,128,256]{2,1,0:T(8,128)(2,1)} %feat_ref.1, s32[32,128]{1,0:T(8,128)} %rows_ref.1), custom_call_target="tpu_custom_call" | custom-call | bytes 6291456 | tf_op jit(solution)/shard_map/pack/pallas_call | solution.py:89
  4.1 0.0 copy-start.4
  4.1 0.0 copy-start.5
  4.1 11.0 %all-to-all-start = ((bf16[32,272,256]{2,1,0:T(8,128)(2,1)}), bf16[32,272,256]{2,1,0:T(8,128)(2,1)}, u32[]{:S(2)}, u32[]{:S(2)}) async-start(bf16[32,272,256]{2,1,0:T(8,128)(2,1)} %bitcast.7), calls=%async_computation | async-start | bytes 8912896 | tf_op jit(solution)/shard_map/all_to_all | solution.py:733
  15.2 1.3 fusion.4
  16.4 3.7 %collective-permute-start = (bf16[1,32,32,256]{3,2,1,0:T(8,128)(2,1)S(1)}, bf16[1,32,32,256]{3,2,1,0:T(8,128)(2,1)S(1)}, u32[]{:S(2)}, u32[]{:S(2)}) collective-permute-start(bf16[1,32,32,256]{3,2,1,0:T(8,128)(2,1)S(1)} %get-tuple-element.7), channel_id=1, source_target_pairs={{0,4},{4,8},{8,12},{12,16},{16,20},{20,24},{24,28},{28,32},{32,36}... | collective-permute-start | bytes 1572872 | tf_op jit(solution)/shard_map/ppermute | solution.py:729
  20.1 1.3 collective-permute-start.1
  21.4 0.0 copy-done.4
  21.4 0.0 copy-done.5
  21.4 0.1 pad_maximum_fusion.w_ref
  21.5 56.3 %collective-permute-done.before_ref = bf16[1,32,32,256]{3,2,1,0:T(8,128)(2,1)S(1)} collective-permute-done((bf16[1,32,32,256]{3,2,1,0:T(8,128)(2,1)S(1)}, bf16[1,32,32,256]{3,2,1,0:T(8,128)(2,1)S(1)}, u32[]{:S(2)}, u32[]{:S(2)}) %collective-permute-start) | collective-permute-done | bytes 524320 | tf_op jit(solution)/shard_map/ppermute | solution.py:729
  77.8 0.0 collective-permute-done.1.after_ref
  77.8 0.8 copy-done.6
  78.6 0.8 copy-done.7
  79.4 26.4 %conv.1.base_ref = f32[16384,128]{1,0:T(8,128)} custom-call(bf16[8,32,32,256]{3,2,1,0:T(8,128)(2,1)} %tokens_ref.1, bf16[1,32,32,256]{3,2,1,0:T(8,128)(2,1)} %copy-done.6, bf16[1,32,32,256]{3,2,1,0:T(8,128)(2,1)} %copy-done.7, f32[27,256]{1,0:T(8,128)} %w_ref.1), custom_call_target="tpu_custom_call" | custom-call | flops 113246208 | bytes 31457280 | tf_op jit(solution)/shard_map/conv/pallas_call | solution.py:166
  105.8 0.0 all-to-all-done
  105.8 0.0 copy-start.2
  105.8 13.4 %scatter.1.mixed_ref = bf16[8192,256]{1,0:T(8,128)(2,1)} custom-call(f32[16384,128]{1,0:T(8,128)} %conv.1.base_ref, bf16[64,136,256]{2,1,0:T(8,128)(2,1)} %bitcast.2.recv_ref), custom_call_target="tpu_custom_call" | custom-call | flops 2097152 | bytes 16777216 | tf_op jit(solution)/shard_map/scatter/pallas_call | solution.py:325
  119.3 0.0 copy-done
  119.3 0.0 copy-done.1
  119.3 0.0 copy-start.3
  119.3 92.4 %mix.1 = (bf16[8192,128]{1,0:T(8,128)(2,1)S(1)}, f32[128,256]{1,0:T(8,128)S(1)}) custom-call(bf16[8192,256]{1,0:T(8,128)(2,1)} %scatter.1.mixed_ref, bf16[1024,512]{1,0:T(8,128)(2,1)S(1)} %pad_maximum_fusion.w_ref, bf16[128,1024]{1,0:T(8,128)(2,1)S(1)} %copy-done, f32[1,1024]{1,0:T(1,128)S(1)} %bitcast.6, f32[128,256]{1,0:T(8,128)S(1)} %copy-done.1), custom_call_target="tpu_custom_call" | custom-call | flops 10737418240 | bytes 16777216 | tf_op jit(solution)/shard_map/mix/pallas_call | solution.py:659
  211.7 3.3 %add_convert_fusion = bf16[8192,256]{1,0:T(8,128)(2,1)} fusion(bf16[8192,256]{1,0:T(8,128)(2,1)S(1)} %copy-done.3, bf16[8192,128]{1,0:T(8,128)(2,1)S(1)} %get-tuple-element.4, f32[128,256]{1,0:T(8,128)S(1)} %get-tuple-element.11), kind=kOutput, calls=%fused_computation | convolution fusion | flops 543195136 | bytes 10616832 | tf_op jit(solution)/shard_map/dot_general | solution.py:747
  214.9 0.7 copy.13
  (6 shorter events, 0.0 us)
Async XLA Ops:
  4.1 17.3 %copy-start.4 = (bf16[1024,256]{1,0:T(8,128)(2,1)S(1)}, bf16[1024,256]{1,0:T(8,128)(2,1)}, u32[]{:S(2)}) copy-start(bf16[1024,256]{1,0:T(8,128)(2,1)} %param.17) | copy-start | bytes 1572868
  4.1 17.3 %copy-start.5 = (bf16[1024,256]{1,0:T(8,128)(2,1)S(1)}, bf16[1024,256]{1,0:T(8,128)(2,1)}, u32[]{:S(2)}) copy-start(bf16[1024,256]{1,0:T(8,128)(2,1)} %param.16) | copy-start | bytes 1572868
  4.1 101.7 %all-to-all-start = ((bf16[32,272,256]{2,1,0:T(8,128)(2,1)}), bf16[32,272,256]{2,1,0:T(8,128)(2,1)}, u32[]{:S(2)}, u32[]{:S(2)}) async-start(bf16[32,272,256]{2,1,0:T(8,128)(2,1)} %bitcast.7), calls=%async_computation | async-start | bytes 8912896 | tf_op jit(solution)/shard_map/all_to_all | solution.py:733
  16.4 61.3 %collective-permute-start = (bf16[1,32,32,256]{3,2,1,0:T(8,128)(2,1)S(1)}, bf16[1,32,32,256]{3,2,1,0:T(8,128)(2,1)S(1)}, u32[]{:S(2)}, u32[]{:S(2)}) collective-permute-start(bf16[1,32,32,256]{3,2,1,0:T(8,128)(2,1)S(1)} %get-tuple-element.7), channel_id=1, source_target_pairs={{0,4},{4,8},{8,12},{12,16},{16,20},{20,24},{24,28},{28,32},{32,36}... | collective-permute-start | bytes 1572872 | tf_op jit(solution)/shard_map/ppermute | solution.py:729
  20.1 57.7 %collective-permute-start.1 = (bf16[1,32,32,256]{3,2,1,0:T(8,128)(2,1)S(1)}, bf16[1,32,32,256]{3,2,1,0:T(8,128)(2,1)S(1)}, u32[]{:S(2)}, u32[]{:S(2)}) collective-permute-start(bf16[1,32,32,256]{3,2,1,0:T(8,128)(2,1)S(1)} %get-tuple-element.6), channel_id=1, source_target_pairs={{4,0},{8,4},{12,8},{16,12},{20,16},{24,20},{28,24},{32,28},{36,32}... | collective-permute-start | bytes 1572872 | tf_op jit(solution)/shard_map/ppermute | solution.py:730
  77.8 0.8 copy-start.6
  78.6 0.8 copy-start.7
  105.8 13.5 %copy-start = (bf16[128,1024]{1,0:T(8,128)(2,1)S(1)}, bf16[128,1024]{1,0:T(8,128)(2,1)}, u32[]{:S(2)}) copy-start(bf16[128,1024]{1,0:T(8,128)(2,1)} %keys_ref.1) | copy-start | bytes 786436
  105.8 13.5 %copy-start.1 = (f32[128,256]{1,0:T(8,128)S(1)}, f32[128,256]{1,0:T(8,128)}, u32[]{:S(2)}) copy-start(f32[128,256]{1,0:T(8,128)} %latents_ref.1) | copy-start | bytes 393220
  105.8 13.5 %copy-start.2 = (f32[1024]{0:T(1024)S(1)}, f32[1024]{0:T(1024)}, u32[]{:S(2)}) copy-start(f32[1024]{0:T(1024)} %param.15) | copy-start | bytes 12292
  119.3 92.4 %copy-start.3 = (bf16[8192,256]{1,0:T(8,128)(2,1)S(1)}, bf16[8192,256]{1,0:T(8,128)(2,1)}, u32[]{:S(2)}) copy-start(bf16[8192,256]{1,0:T(8,128)(2,1)} %scatter.1.mixed_ref) | copy-start | bytes 12582916

commit v6 on v5

--- a/solution.py
+++ b/solution.py
@@ -19,9 +19,9 @@
 
 
 def pack_kernel(
-    capacity, empty, dest_ref, feat_ref, rows_ref, out_ref, taken, slot_of, feat, codes, in_sems, out_sems, code_sem
+    capacity, empty, dest_ref, feat_ref, rows_ref, out_ref, taken, turn_of, feat, wide, codes, in_sems, out_sems, code_sem
 ):
-    slots, _, width = out_ref.shape
+    slabs, _, width = out_ref.shape
     blocks, rows, _ = feat_ref.shape
     pieces = in_sems.shape[0]
     each = blocks // pieces
@@ -35,35 +35,32 @@
 
     def coded(number):
         both = jnp.concatenate([number // 128, number % 128], axis=1)
-        return jnp.broadcast_to(both.astype(F32), (EXTRA, width)).astype(BF16)
-
-    nothing = coded(jnp.full((1, rows), empty, jnp.int32))
-
-    def clear(j, carry):
-        codes[j] = nothing
-        return carry
-
-    lax.fori_loop(0, slots, clear, 0)
-    for t in range(slots // capacity):
+        return both.astype(F32)
+
+    wide[...] = jnp.broadcast_to(coded(jnp.full((1, rows), empty, jnp.int32)), wide.shape)
+    for t in range(slabs):
         taken[t] = 0
 
     def place(b, carry):
         to = dest_ref[b]
-        slot = to * capacity + taken[to]
-        taken[to] = taken[to] + 1
-        slot_of[b] = slot
-        codes[slot] = coded(rows_ref[pl.ds(b, 1), :])
+        turn = taken[to]
+        taken[to] = turn + 1
+        turn_of[b] = turn
+        wide[pl.ds(to * EXTRA + turn, 1), :] = coded(rows_ref[pl.ds(b, 1), :])
         return carry
 
     lax.fori_loop(0, blocks, place, 0)
+    codes[...] = wide[...].reshape(slabs, EXTRA, width).astype(BF16)
     code_copy = pltpu.make_async_copy(
-        codes, out_ref.at[pl.ds(0, slots), pl.ds(rows, EXTRA)], code_sem
+        codes, out_ref.at[pl.ds(0, slabs), pl.ds(capacity * rows, EXTRA)], code_sem
     )
     code_copy.start()
 
     def put(b):
         return pltpu.make_async_copy(
-            feat.at[b], out_ref.at[slot_of[b], pl.ds(0, rows)], out_sems.at[b]
+            feat.at[b],
+            out_ref.at[dest_ref[b], pl.ds(pl.multiple_of(turn_of[b] * rows, rows), rows)],
+            out_sems.at[b],
         )
 
     def send(b, carry):
@@ -83,19 +80,19 @@
 
 def pack(dest, feat, row_ids, slabs, capacity, empty):
     blocks, rows, width = feat.shape
-    slots = slabs * capacity
     anywhere = pl.BlockSpec(memory_space=pl.ANY)
     dma = pltpu.SemaphoreType.DMA
     return pl.pallas_call(
         functools.partial(pack_kernel, capacity, empty),
-        out_shape=jax.ShapeDtypeStruct((slots, rows + EXTRA, width), BF16),
+        out_shape=jax.ShapeDtypeStruct((slabs, capacity * rows + EXTRA, width), BF16),
         in_specs=[pl.BlockSpec(memory_space=pltpu.SMEM), anywhere, whole()],
         out_specs=anywhere,
         scratch_shapes=[
             pltpu.SMEM((slabs,), jnp.int32),
             pltpu.SMEM((blocks,), jnp.int32),
             pltpu.VMEM(feat.shape, BF16),
-            pltpu.VMEM((slots, EXTRA, width), BF16),
+            pltpu.VMEM((slabs * EXTRA, width), F32),
+            pltpu.VMEM((slabs, EXTRA, width), BF16),
             dma((4,)),
             dma((blocks,)),
             dma,
@@ -199,20 +196,25 @@
     out_sems,
 ):
     slots, block_rows, _ = feat.shape
+    slabs = recv_ref.shape[0]
+    capacity = slots // slabs
     total = acc.shape[0] // 2
     pieces = feat_sems.shape[0]
     each = slots // pieces
     step = 128
 
     code_copy = pltpu.make_async_copy(
-        recv_ref.at[pl.ds(0, slots), pl.ds(block_rows, EXTRA)], codes, code_sems.at[0]
+        recv_ref.at[pl.ds(0, slabs), pl.ds(capacity * block_rows, EXTRA)], codes, code_sems.at[0]
     )
     code_copy.start()
     base_copy = pltpu.make_async_copy(base_ref, acc, base_sem)
 
     def fetch(i):
         return pltpu.make_async_copy(
-            recv_ref.at[pl.ds(i * each, each), pl.ds(0, block_rows)],
+            recv_ref.at[
+                pl.ds(i * each % slabs, each),
+                pl.ds(pl.multiple_of(i * each // slabs * block_rows, block_rows), block_rows),
+            ],
             feat.at[pl.ds(i * each, each)],
             feat_sems.at[i],
         )
@@ -222,7 +224,11 @@
         fetch(i).start()
 
     code_copy.wait()
-    code = jnp.max(codes[...].astype(F32), axis=1)
+    coded = codes[...].astype(F32)
+    turn = lax.broadcasted_iota(jnp.int32, coded.shape, 1)
+    code = jnp.concatenate(
+        [jnp.max(jnp.where(turn == k, coded, 0.0), axis=1) for k in range(capacity)], axis=0
+    )
     number = (code[:, :block_rows] * 128.0 + code[:, block_rows:]).astype(jnp.int32)
     spots[...] = (number // 8) * 16 + number % 8
     lane = lax.broadcasted_iota(jnp.int32, number.shape, 1)
@@ -317,9 +323,9 @@
         out_copy(p).wait()
 
 
-def scatter(base, recv):
+def scatter(base, recv, capacity):
     total, width = base.shape[0] // 2, 2 * base.shape[1]
-    slots, block_rows = recv.shape[0], recv.shape[1] - EXTRA
+    slots, block_rows = capacity * recv.shape[0], (recv.shape[1] - EXTRA) // capacity
     anywhere = pl.BlockSpec(memory_space=pl.ANY)
     dma = pltpu.SemaphoreType.DMA
     return pl.pallas_call(
@@ -331,7 +337,7 @@
             pltpu.VMEM((2 * total, 128), F32),
             pltpu.VMEM((2 * block_rows, 128), F32),
             pltpu.VMEM((slots, block_rows, width), BF16),
-            pltpu.VMEM((slots, EXTRA, width), BF16),
+            pltpu.VMEM((recv.shape[0], EXTRA, width), BF16),
             pltpu.VMEM((slots, block_rows), jnp.int32),
             pltpu.VMEM((slots, block_rows), jnp.int32),
             pltpu.VMEM((total, width), BF16),
@@ -720,9 +726,8 @@
     depth, side_y, side_x, width = tokens.shape
     row_count = depth * side_y * side_x
     slabs = lax.axis_size("slab")
-    blocks, block_rows = refine_rows.shape
+    blocks, _ = refine_rows.shape
     capacity = max(2, (2 * blocks + slabs - 1) // slabs)
-    slots = slabs * capacity
 
     up = [(i, i + 1) for i in range(slabs - 1)]
     down = [(i + 1, i) for i in range(slabs - 1)]
@@ -731,18 +736,17 @@
 
     sent = pack(refine_dest[:, 0], refine_feat, refine_rows, slabs, capacity, row_count)
     received = lax.all_to_all(
-        sent.reshape(slabs, capacity * (block_rows + EXTRA), width),
+        sent,
         "slab",
         split_axis=0,
         concat_axis=0,
         tiled=True,
     )
-    received = received.reshape(slots, block_rows + EXTRA, width)
 
     base = conv(tokens, before, after, conv_w)
     weights = jnp.concatenate([w_val, w_gate], axis=1)
 
-    mixed = scatter(base, received)
+    mixed = scatter(base, received, capacity)
     assign, latent_new = mix(mixed, weights, latent_keys, norm_gain[None, :], latents)
     readback = jnp.dot(assign, latent_new.astype(BF16), preferred_element_type=F32)
     block_out = (mixed.astype(F32) + readback).astype(BF16)

time: 218 us -> 216 us (level)
  no operation moved by 1% of the time
where the time goes in v6:
time: 216 us; the launch traced here: 213 us
  Pallas kernels  135 us (62%)
  waiting for transfers between devices  54.6 us (25%)
  starting transfers between devices  15.9 us (7%)
  local copies, waits for them, and re-layouts  3.55 us (2%)
  matrix products  3.25 us (2%)
    pallas_call x1, Pallas kernels, mix(): pl.pallas_call(mix_kernel, out_shape=(jax.ShapeDtypeStruct((rows, held),...  92 us
    ppermute x1, waiting for transfers between devices, per_device(): before = lax.ppermute(tokens[-1:], 'slab', up)  54.6 us
    pallas_call x1, Pallas kernels, conv(): pl.pallas_call(conv_kernel, grid=(depth,), out_shape=jax.ShapeDtypeStruct...  26.4 us
    pallas_call x1, Pallas kernels, scatter(): pl.pallas_call(scatter_kernel, out_shape=jax.ShapeDtypeStruct((total, wid...  13.4 us
    all_to_all x1, starting transfers between devices, per_device(): lax.all_to_all(sent, 'slab', split_axis=0, concat_axis=0, tiled=True)  11 us
  transfers between devices with their start and end apart: 3, of which 1 were waited for; matrix products, arithmetic and copies ran while one was open for 1% of the time, Pallas kernels for 12%

profile of v6, /device:TPU:0, one launch (start us, length us, event | category | flops | bytes accessed | tf_op | source)
XLA Modules:
  0.0 213.4 jit_solution(4652464151914221184)
XLA Ops:
  0.6 3.5 %pack.1 = bf16[32,264,256]{2,1,0:T(8,128)(2,1)} custom-call(s32[32]{0:T(128)} %bitcast.6, bf16[32,128,256]{2,1,0:T(8,128)(2,1)} %feat_ref.1, s32[32,128]{1,0:T(8,128)} %rows_ref.1), custom_call_target="tpu_custom_call" | custom-call | bytes 6291456 | tf_op jit(solution)/shard_map/pack/pallas_call | solution.py:85
  4.1 0.0 copy-start.4
  4.1 0.0 copy-start.5
  4.1 11.0 %all-to-all-start = ((bf16[32,264,256]{2,1,0:T(8,128)(2,1)}), bf16[32,264,256]{2,1,0:T(8,128)(2,1)}, u32[]{:S(2)}, u32[]{:S(2)}) async-start(bf16[32,264,256]{2,1,0:T(8,128)(2,1)} %pack.1), calls=%async_computation | async-start | bytes 8650752 | tf_op jit(solution)/shard_map/all_to_all | solution.py:738
  15.1 1.3 fusion.4
  16.4 3.7 %collective-permute-start = (bf16[1,32,32,256]{3,2,1,0:T(8,128)(2,1)S(1)}, bf16[1,32,32,256]{3,2,1,0:T(8,128)(2,1)S(1)}, u32[]{:S(2)}, u32[]{:S(2)}) collective-permute-start(bf16[1,32,32,256]{3,2,1,0:T(8,128)(2,1)S(1)} %get-tuple-element.7), channel_id=1, source_target_pairs={{0,4},{4,8},{8,12},{12,16},{16,20},{20,24},{24,28},{28,32},{32,36}... | collective-permute-start | bytes 1572872 | tf_op jit(solution)/shard_map/ppermute | solution.py:734
  20.1 1.3 collective-permute-start.1
  21.4 0.0 copy-done.4
  21.4 0.0 copy-done.5
  21.4 0.1 pad_maximum_fusion.w_ref
  21.5 54.6 %collective-permute-done.before_ref = bf16[1,32,32,256]{3,2,1,0:T(8,128)(2,1)S(1)} collective-permute-done((bf16[1,32,32,256]{3,2,1,0:T(8,128)(2,1)S(1)}, bf16[1,32,32,256]{3,2,1,0:T(8,128)(2,1)S(1)}, u32[]{:S(2)}, u32[]{:S(2)}) %collective-permute-start) | collective-permute-done | bytes 524320 | tf_op jit(solution)/shard_map/ppermute | solution.py:734
  76.0 0.0 collective-permute-done.1.after_ref
  76.0 0.8 copy-done.6
  76.8 0.8 copy-done.7
  77.6 26.4 %conv.1.base_ref = f32[16384,128]{1,0:T(8,128)} custom-call(bf16[8,32,32,256]{3,2,1,0:T(8,128)(2,1)} %tokens_ref.1, bf16[1,32,32,256]{3,2,1,0:T(8,128)(2,1)} %copy-done.6, bf16[1,32,32,256]{3,2,1,0:T(8,128)(2,1)} %copy-done.7, f32[27,256]{1,0:T(8,128)} %w_ref.1), custom_call_target="tpu_custom_call" | custom-call | flops 113246208 | bytes 31457280 | tf_op jit(solution)/shard_map/conv/pallas_call | solution.py:163
  104.1 0.0 all-to-all-done.recv_ref
  104.1 13.4 %scatter.1.mixed_ref = bf16[8192,256]{1,0:T(8,128)(2,1)} custom-call(f32[16384,128]{1,0:T(8,128)} %conv.1.base_ref, bf16[32,264,256]{2,1,0:T(8,128)(2,1)} %all-to-all-done.recv_ref), custom_call_target="tpu_custom_call" | custom-call | flops 2097152 | bytes 16777216 | tf_op jit(solution)/shard_map/scatter/pallas_call | solution.py:331
  117.5 0.0 copy-done
  117.5 0.0 copy-done.1
  117.5 0.0 copy-done.2
  117.5 0.0 copy-start.3
  117.5 92.0 %mix.1 = (bf16[8192,128]{1,0:T(8,128)(2,1)S(1)}, f32[128,256]{1,0:T(8,128)S(1)}) custom-call(bf16[8192,256]{1,0:T(8,128)(2,1)} %scatter.1.mixed_ref, bf16[1024,512]{1,0:T(8,128)(2,1)S(1)} %pad_maximum_fusion.w_ref, bf16[128,1024]{1,0:T(8,128)(2,1)S(1)} %copy-done, f32[1,1024]{1,0:T(1,128)S(1)} %bitcast.4, f32[128,256]{1,0:T(8,128)S(1)} %copy-done.1), custom_call_target="tpu_custom_call" | custom-call | flops 10737418240 | bytes 16777216 | tf_op jit(solution)/shard_map/mix/pallas_call | solution.py:665
  209.5 3.3 %add_convert_fusion = bf16[8192,256]{1,0:T(8,128)(2,1)} fusion(bf16[8192,256]{1,0:T(8,128)(2,1)S(1)} %copy-done.3, bf16[8192,128]{1,0:T(8,128)(2,1)S(1)} %get-tuple-element.4, f32[128,256]{1,0:T(8,128)S(1)} %get-tuple-element.11), kind=kOutput, calls=%fused_computation | convolution fusion | flops 543195136 | bytes 10616832 | tf_op jit(solution)/shard_map/dot_general | solution.py:751
  212.7 0.7 copy.13
  (6 shorter events, 0.0 us)
Async XLA Ops:
  4.1 17.2 %copy-start.4 = (bf16[1024,256]{1,0:T(8,128)(2,1)S(1)}, bf16[1024,256]{1,0:T(8,128)(2,1)}, u32[]{:S(2)}) copy-start(bf16[1024,256]{1,0:T(8,128)(2,1)} %param.17) | copy-start | bytes 1572868
  4.1 17.2 %copy-start.5 = (bf16[1024,256]{1,0:T(8,128)(2,1)S(1)}, bf16[1024,256]{1,0:T(8,128)(2,1)}, u32[]{:S(2)}) copy-start(bf16[1024,256]{1,0:T(8,128)(2,1)} %param.16) | copy-start | bytes 1572868
  4.1 99.9 %all-to-all-start = ((bf16[32,264,256]{2,1,0:T(8,128)(2,1)}), bf16[32,264,256]{2,1,0:T(8,128)(2,1)}, u32[]{:S(2)}, u32[]{:S(2)}) async-start(bf16[32,264,256]{2,1,0:T(8,128)(2,1)} %pack.1), calls=%async_computation | async-start | bytes 8650752 | tf_op jit(solution)/shard_map/all_to_all | solution.py:738
  16.4 59.6 %collective-permute-start = (bf16[1,32,32,256]{3,2,1,0:T(8,128)(2,1)S(1)}, bf16[1,32,32,256]{3,2,1,0:T(8,128)(2,1)S(1)}, u32[]{:S(2)}, u32[]{:S(2)}) collective-permute-start(bf16[1,32,32,256]{3,2,1,0:T(8,128)(2,1)S(1)} %get-tuple-element.7), channel_id=1, source_target_pairs={{0,4},{4,8},{8,12},{12,16},{16,20},{20,24},{24,28},{28,32},{32,36}... | collective-permute-start | bytes 1572872 | tf_op jit(solution)/shard_map/ppermute | solution.py:734
  20.1 56.0 %collective-permute-start.1 = (bf16[1,32,32,256]{3,2,1,0:T(8,128)(2,1)S(1)}, bf16[1,32,32,256]{3,2,1,0:T(8,128)(2,1)S(1)}, u32[]{:S(2)}, u32[]{:S(2)}) collective-permute-start(bf16[1,32,32,256]{3,2,1,0:T(8,128)(2,1)S(1)} %get-tuple-element.6), channel_id=1, source_target_pairs={{4,0},{8,4},{12,8},{16,12},{20,16},{24,20},{28,24},{32,28},{36,32}... | collective-permute-start | bytes 1572872 | tf_op jit(solution)/shard_map/ppermute | solution.py:735
  76.0 0.8 copy-start.6
  76.8 0.8 copy-start.7
  104.1 13.4 %copy-start = (bf16[128,1024]{1,0:T(8,128)(2,1)S(1)}, bf16[128,1024]{1,0:T(8,128)(2,1)}, u32[]{:S(2)}) copy-start(bf16[128,1024]{1,0:T(8,128)(2,1)} %keys_ref.1) | copy-start | bytes 786436
  104.1 13.4 %copy-start.1 = (f32[128,256]{1,0:T(8,128)S(1)}, f32[128,256]{1,0:T(8,128)}, u32[]{:S(2)}) copy-start(f32[128,256]{1,0:T(8,128)} %latents_ref.1) | copy-start | bytes 393220
  104.1 13.4 %copy-start.2 = (f32[1024]{0:T(1024)S(1)}, f32[1024]{0:T(1024)}, u32[]{:S(2)}) copy-start(f32[1024]{0:T(1024)} %param.15) | copy-start | bytes 12292
  117.5 92.0 %copy-start.3 = (bf16[8192,256]{1,0:T(8,128)(2,1)S(1)}, bf16[8192,256]{1,0:T(8,128)(2,1)}, u32[]{:S(2)}) copy-start(bf16[8192,256]{1,0:T(8,128)(2,1)} %scatter.1.mixed_ref) | copy-start | bytes 12582916

commit v7 on v6

--- a/solution.py
+++ b/solution.py
@@ -520,6 +520,7 @@
         return carry
 
     lax.fori_loop(0, CHUNKS // 2, early, 0)
+    a_copy(1, 0).start()
     w_copy(1).wait_recv()
     w_copy(2).start()
     w_copy(0).wait_recv()
@@ -559,8 +560,8 @@
     for n in (4, 1, 2, 5, 6, 3, 0):
         p_copy(n).start()
     for i in range(2):
-        for d in (2, 1):
-            a_copy(d, i).start()
+        a_copy(2, i).start()
+    a_copy(1, 1).start()
     keep = pltpu.make_async_copy(own, assign_ref.at[pl.ds(chan * quarter, quarter)], local_sem.at[0])
     keep.start()
     part_in[place] = part_out[chan]

time: 216 us -> 216 us (level)
  no operation moved by 1% of the time
where the time goes in v7:
time: 216 us; the launch traced here: 213 us
  Pallas kernels  135 us (62%)
  waiting for transfers between devices  54.6 us (25%)
  starting transfers between devices  15.9 us (7%)
  local copies, waits for them, and re-layouts  3.55 us (2%)
  matrix products  3.25 us (2%)
    pallas_call x1, Pallas kernels, mix(): pl.pallas_call(mix_kernel, out_shape=(jax.ShapeDtypeStruct((rows, held),...  92 us
    ppermute x1, waiting for transfers between devices, per_device(): before = lax.ppermute(tokens[-1:], 'slab', up)  54.6 us
    pallas_call x1, Pallas kernels, conv(): pl.pallas_call(conv_kernel, grid=(depth,), out_shape=jax.ShapeDtypeStruct...  26.4 us
    pallas_call x1, Pallas kernels, scatter(): pl.pallas_call(scatter_kernel, out_shape=jax.ShapeDtypeStruct((total, wid...  13.4 us
    all_to_all x1, starting transfers between devices, per_device(): lax.all_to_all(sent, 'slab', split_axis=0, concat_axis=0, tiled=True)  11 us
  transfers between devices with their start and end apart: 3, of which 1 were waited for; matrix products, arithmetic and copies ran while one was open for 1% of the time, Pallas kernels for 12%

profile of v7, /device:TPU:0, one launch (start us, length us, event | category | flops | bytes accessed | tf_op | source)
XLA Modules:
  0.0 213.4 jit_solution(6272168861032143717)
XLA Ops:
  0.6 3.5 %pack.1 = bf16[32,264,256]{2,1,0:T(8,128)(2,1)} custom-call(s32[32]{0:T(128)} %bitcast.6, bf16[32,128,256]{2,1,0:T(8,128)(2,1)} %feat_ref.1, s32[32,128]{1,0:T(8,128)} %rows_ref.1), custom_call_target="tpu_custom_call" | custom-call | bytes 6291456 | tf_op jit(solution)/shard_map/pack/pallas_call | solution.py:85
  4.1 0.0 copy-start.4
  4.1 0.0 copy-start.5
  4.1 11.0 %all-to-all-start = ((bf16[32,264,256]{2,1,0:T(8,128)(2,1)}), bf16[32,264,256]{2,1,0:T(8,128)(2,1)}, u32[]{:S(2)}, u32[]{:S(2)}) async-start(bf16[32,264,256]{2,1,0:T(8,128)(2,1)} %pack.1), calls=%async_computation | async-start | bytes 8650752 | tf_op jit(solution)/shard_map/all_to_all | solution.py:739
  15.1 1.3 fusion.4
  16.4 3.7 %collective-permute-start = (bf16[1,32,32,256]{3,2,1,0:T(8,128)(2,1)S(1)}, bf16[1,32,32,256]{3,2,1,0:T(8,128)(2,1)S(1)}, u32[]{:S(2)}, u32[]{:S(2)}) collective-permute-start(bf16[1,32,32,256]{3,2,1,0:T(8,128)(2,1)S(1)} %get-tuple-element.7), channel_id=1, source_target_pairs={{0,4},{4,8},{8,12},{12,16},{16,20},{20,24},{24,28},{28,32},{32,36}... | collective-permute-start | bytes 1572872 | tf_op jit(solution)/shard_map/ppermute | solution.py:735
  20.1 1.3 collective-permute-start.1
  21.4 0.0 copy-done.4
  21.4 0.0 copy-done.5
  21.4 0.1 pad_maximum_fusion.w_ref
  21.5 54.6 %collective-permute-done.before_ref = bf16[1,32,32,256]{3,2,1,0:T(8,128)(2,1)S(1)} collective-permute-done((bf16[1,32,32,256]{3,2,1,0:T(8,128)(2,1)S(1)}, bf16[1,32,32,256]{3,2,1,0:T(8,128)(2,1)S(1)}, u32[]{:S(2)}, u32[]{:S(2)}) %collective-permute-start) | collective-permute-done | bytes 524320 | tf_op jit(solution)/shard_map/ppermute | solution.py:735
  76.0 0.0 collective-permute-done.1.after_ref
  76.0 0.8 copy-done.6
  76.8 0.8 copy-done.7
  77.6 26.4 %conv.1.base_ref = f32[16384,128]{1,0:T(8,128)} custom-call(bf16[8,32,32,256]{3,2,1,0:T(8,128)(2,1)} %tokens_ref.1, bf16[1,32,32,256]{3,2,1,0:T(8,128)(2,1)} %copy-done.6, bf16[1,32,32,256]{3,2,1,0:T(8,128)(2,1)} %copy-done.7, f32[27,256]{1,0:T(8,128)} %w_ref.1), custom_call_target="tpu_custom_call" | custom-call | flops 113246208 | bytes 31457280 | tf_op jit(solution)/shard_map/conv/pallas_call | solution.py:163
  104.1 0.0 all-to-all-done.recv_ref
  104.1 13.4 %scatter.1.mixed_ref = bf16[8192,256]{1,0:T(8,128)(2,1)} custom-call(f32[16384,128]{1,0:T(8,128)} %conv.1.base_ref, bf16[32,264,256]{2,1,0:T(8,128)(2,1)} %all-to-all-done.recv_ref), custom_call_target="tpu_custom_call" | custom-call | flops 2097152 | bytes 16777216 | tf_op jit(solution)/shard_map/scatter/pallas_call | solution.py:331
  117.5 0.0 copy-done
  117.5 0.0 copy-done.1
  117.5 0.0 copy-done.2
  117.5 0.0 copy-start.3
  117.5 92.0 %mix.1 = (bf16[8192,128]{1,0:T(8,128)(2,1)S(1)}, f32[128,256]{1,0:T(8,128)S(1)}) custom-call(bf16[8192,256]{1,0:T(8,128)(2,1)} %scatter.1.mixed_ref, bf16[1024,512]{1,0:T(8,128)(2,1)S(1)} %pad_maximum_fusion.w_ref, bf16[128,1024]{1,0:T(8,128)(2,1)S(1)} %copy-done, f32[1,1024]{1,0:T(1,128)S(1)} %bitcast.4, f32[128,256]{1,0:T(8,128)S(1)} %copy-done.1), custom_call_target="tpu_custom_call" | custom-call | flops 10737418240 | bytes 16777216 | tf_op jit(solution)/shard_map/mix/pallas_call | solution.py:666
  209.5 3.3 %add_convert_fusion = bf16[8192,256]{1,0:T(8,128)(2,1)} fusion(bf16[8192,256]{1,0:T(8,128)(2,1)S(1)} %copy-done.3, bf16[8192,128]{1,0:T(8,128)(2,1)S(1)} %get-tuple-element.4, f32[128,256]{1,0:T(8,128)S(1)} %get-tuple-element.11), kind=kOutput, calls=%fused_computation | convolution fusion | flops 543195136 | bytes 10616832 | tf_op jit(solution)/shard_map/dot_general | solution.py:752
  212.7 0.7 copy.13
  (6 shorter events, 0.0 us)
Async XLA Ops:
  4.1 17.2 %copy-start.4 = (bf16[1024,256]{1,0:T(8,128)(2,1)S(1)}, bf16[1024,256]{1,0:T(8,128)(2,1)}, u32[]{:S(2)}) copy-start(bf16[1024,256]{1,0:T(8,128)(2,1)} %param.17) | copy-start | bytes 1572868
  4.1 17.2 %copy-start.5 = (bf16[1024,256]{1,0:T(8,128)(2,1)S(1)}, bf16[1024,256]{1,0:T(8,128)(2,1)}, u32[]{:S(2)}) copy-start(bf16[1024,256]{1,0:T(8,128)(2,1)} %param.16) | copy-start | bytes 1572868
  4.1 99.9 %all-to-all-start = ((bf16[32,264,256]{2,1,0:T(8,128)(2,1)}), bf16[32,264,256]{2,1,0:T(8,128)(2,1)}, u32[]{:S(2)}, u32[]{:S(2)}) async-start(bf16[32,264,256]{2,1,0:T(8,128)(2,1)} %pack.1), calls=%async_computation | async-start | bytes 8650752 | tf_op jit(solution)/shard_map/all_to_all | solution.py:739
  16.4 59.6 %collective-permute-start = (bf16[1,32,32,256]{3,2,1,0:T(8,128)(2,1)S(1)}, bf16[1,32,32,256]{3,2,1,0:T(8,128)(2,1)S(1)}, u32[]{:S(2)}, u32[]{:S(2)}) collective-permute-start(bf16[1,32,32,256]{3,2,1,0:T(8,128)(2,1)S(1)} %get-tuple-element.7), channel_id=1, source_target_pairs={{0,4},{4,8},{8,12},{12,16},{16,20},{20,24},{24,28},{28,32},{32,36}... | collective-permute-start | bytes 1572872 | tf_op jit(solution)/shard_map/ppermute | solution.py:735
  20.1 56.0 %collective-permute-start.1 = (bf16[1,32,32,256]{3,2,1,0:T(8,128)(2,1)S(1)}, bf16[1,32,32,256]{3,2,1,0:T(8,128)(2,1)S(1)}, u32[]{:S(2)}, u32[]{:S(2)}) collective-permute-start(bf16[1,32,32,256]{3,2,1,0:T(8,128)(2,1)S(1)} %get-tuple-element.6), channel_id=1, source_target_pairs={{4,0},{8,4},{12,8},{16,12},{20,16},{24,20},{28,24},{32,28},{36,32}... | collective-permute-start | bytes 1572872 | tf_op jit(solution)/shard_map/ppermute | solution.py:736
  76.0 0.8 copy-start.6
  76.8 0.8 copy-start.7
  104.1 13.4 %copy-start = (bf16[128,1024]{1,0:T(8,128)(2,1)S(1)}, bf16[128,1024]{1,0:T(8,128)(2,1)}, u32[]{:S(2)}) copy-start(bf16[128,1024]{1,0:T(8,128)(2,1)} %keys_ref.1) | copy-start | bytes 786436
  104.1 13.4 %copy-start.1 = (f32[128,256]{1,0:T(8,128)S(1)}, f32[128,256]{1,0:T(8,128)}, u32[]{:S(2)}) copy-start(f32[128,256]{1,0:T(8,128)} %latents_ref.1) | copy-start | bytes 393220
  104.1 13.4 %copy-start.2 = (f32[1024]{0:T(1024)S(1)}, f32[1024]{0:T(1024)}, u32[]{:S(2)}) copy-start(f32[1024]{0:T(1024)} %param.15) | copy-start | bytes 12292
  117.5 92.0 %copy-start.3 = (bf16[8192,256]{1,0:T(8,128)(2,1)S(1)}, bf16[8192,256]{1,0:T(8,128)(2,1)}, u32[]{:S(2)}) copy-start(bf16[8192,256]{1,0:T(8,128)(2,1)} %scatter.1.mixed_ref) | copy-start | bytes 12582916
